TPU v7x, 32 devices: a whole 2x2x4 slice. The times are simulated.
32 devices in a mesh: bead: 16 (over z, y, x), space: 2 (over core).
Axes of the slice: x: 2, y: 2, z: 4, core: 2. Of those that a mesh axis runs over, the one named last changes fastest.
Arguments:
- positions: float32 [32, 3, 16384], P('bead', None, 'space'), may hold values from -6 to 6
- momenta: float32 [32, 3, 16384], P('bead', None, 'space'), may hold values from -6 to 6
- forces: float32 [32, 3, 16384], P('bead', None, 'space'), may hold values from -6 to 6
- gle_drift: float32 [32, 5, 5], replicated, may hold values from -0.25 to 0.98, as said below
- gle_noise_mix: float32 [32, 5, 5], replicated, may hold values from -1.5 to 1.5
- aux_momenta: float32 [32, 4, 3, 16384], P(None, None, None, ('space', 'bead')), may hold values from -6 to 6
- noise: float32 [2, 32, 5, 3, 16384], P(None, None, None, None, ('space', 'bead')), may hold values from -6 to 6
Outputs:
- positions_out: float32 [32, 3, 16384], P('bead', None, 'space')
- momenta_out: float32 [32, 3, 16384], P('bead', None, 'space')
- forces_out: float32 [32, 3, 16384], P('bead', None, 'space')
- aux_out: float32 [32, 4, 3, 16384], P(None, None, None, ('space', 'bead'))
Inputs may be any that keep to these rules, and one draw needn't show every extreme that they name: `gle_drift`: one matrix a mode; diagonal entries positive.
All inputs are finite; a program needn't handle non-finite values.
Results may differ from a plain program's by a relative error of at most 0.00012.
Values sent between devices are 32-bit elements; how exact they have to be, the bound alone decides.
No kernel may reach another device: no remote copies, remote signals or barrier semaphores. Data moves between devices by JAX's collectives and lax.ppermute only.
A program may use at most 64 MiB of HBM per device.

v0:
```python
import math

import jax
import jax.numpy as jnp
from jax import lax
from jax.sharding import PartitionSpec as P

BEADS = 32
CELL_ATOMS = 128
STEPS = 2


time_step = 0.5
cycle_freq = 1.5
cell_length = 2.0
pair_strength = 0.1
pair_range = 1.0


def passed_along(block, axis, distance):
    devices = range(lax.axis_size(axis))
    route = [((i - distance) % len(devices), i) for i in devices]
    return lax.ppermute(block, axis, route)


def mode_basis():
    index = jnp.arange(BEADS)
    bead_pos = index.astype(jnp.float32)[:, None]
    mode_pos = index.astype(jnp.float32)[None, :]
    phase = 2.0 * jnp.pi * bead_pos * mode_pos / BEADS
    kk = index[None, :]
    low = jnp.sqrt(1.0 / BEADS) + 0.0 * phase
    basis = jnp.where(
        kk == 0,
        low,
        jnp.where(
            kk < BEADS // 2,
            jnp.sqrt(2.0 / BEADS) * jnp.cos(phase),
            jnp.where(
                kk == BEADS // 2,
                jnp.sqrt(1.0 / BEADS) * jnp.cos(phase),
                jnp.sqrt(2.0 / BEADS) * jnp.sin(phase),
            ),
        ),
    )
    freq = 2.0 * cycle_freq * jnp.sin(jnp.pi * index.astype(jnp.float32) / BEADS)
    return (basis, freq, index)


def tile_weight(center, other):
    sa = jnp.sum(center * center, axis=1)
    sb = jnp.sum(other * other, axis=1)
    cross = jnp.einsum("xcni,xcnj->xnij", center, other, precision=lax.Precision.HIGHEST)
    dist = sa[:, :, :, None] + sb[:, :, None, :] - 2.0 * cross
    return jnp.exp(-dist / (2.0 * pair_range))


def pull(center, other):
    weight = tile_weight(center, other)
    rowsum = jnp.sum(weight, axis=3)
    pulled = jnp.einsum("xnij,xcnj->xcni", weight, other, precision=lax.Precision.HIGHEST)
    return pair_strength / pair_range * (center * rowsum[:, None] - pulled)


def mutual(center, other):
    weight = tile_weight(center, other)
    rowsum = jnp.sum(weight, axis=3)
    colsum = jnp.sum(weight, axis=2)
    pulled = jnp.einsum("xnij,xcnj->xcni", weight, other, precision=lax.Precision.HIGHEST)
    pushed = jnp.einsum("xnij,xcni->xcnj", weight, center, precision=lax.Precision.HIGHEST)
    coef = pair_strength / pair_range
    return (coef * (center * rowsum[:, None] - pulled), coef * (other * colsum[:, None] - pushed))


def moved(cells, delta):
    offset = jnp.asarray([delta * cell_length, 0.0, 0.0], dtype=cells.dtype).reshape(1, 3, 1, 1)
    return cells + offset


def pair_forces(positions):
    beads_here = positions.shape[0]
    cells = positions.shape[2] // CELL_ATOMS
    block = math.gcd(cells, 16)
    following = passed_along(positions[:, :, :CELL_ATOMS], "space", -1)
    grid = jnp.concatenate([positions, following], axis=2).reshape(
        beads_here, 3, cells + 1, CELL_ATOMS
    )

    def accumulate_pairs(number, total):
        start = number * block
        center = lax.dynamic_slice_in_dim(grid, start, block, 2)
        other = lax.dynamic_slice_in_dim(grid, start + 1, block, 2)
        own = pull(center, center)
        on_center, on_other = mutual(center, moved(other, 1))
        total = lax.dynamic_update_slice_in_dim(
            total, lax.dynamic_slice_in_dim(total, start, block, 2) + own + on_center, start, 2
        )
        return lax.dynamic_update_slice_in_dim(
            total, lax.dynamic_slice_in_dim(total, start + 1, block, 2) + on_other, start + 1, 2
        )

    total = jnp.zeros((beads_here, 3, cells + 1, CELL_ATOMS), positions.dtype)
    total = lax.fori_loop(0, cells // block, accumulate_pairs, total)
    returned = passed_along(total[:, :, cells], "space", 1)
    first = total[:, :, 0] + returned
    result = jnp.concatenate([first[:, :, None], total[:, :, 1:cells]], axis=2)
    return result.reshape(positions.shape)


def mode_step(qbeads, pbeads, aux, noise_now, basis, cosine, sinc, wsin, gle_drift, gle_noise_mix):
    qmode = jnp.einsum("jk,jcn->kcn", basis, qbeads, precision=lax.Precision.HIGHEST)
    pmode = jnp.einsum("jk,jcn->kcn", basis, pbeads, precision=lax.Precision.HIGHEST)
    state = jnp.concatenate([pmode[:, None], aux], axis=1)
    state = jnp.einsum(
        "kab,kbcn->kacn", gle_drift, state, precision=lax.Precision.HIGHEST
    ) + jnp.einsum("kab,kbcn->kacn", gle_noise_mix, noise_now, precision=lax.Precision.HIGHEST)
    pmode = state[:, 0]
    qnext = qmode * cosine + sinc * pmode
    pmode = pmode * cosine - wsin * qmode
    qbeads = jnp.einsum("jk,kcn->jcn", basis, qnext, precision=lax.Precision.HIGHEST)
    pbeads = jnp.einsum("jk,kcn->jcn", basis, pmode, precision=lax.Precision.HIGHEST)
    return (qbeads, pbeads, state[:, 1:])


def on_device(positions, momenta, forces, gle_drift, gle_noise_mix, aux_momenta, noise):
    beads_here = positions.shape[0]
    atoms_here = positions.shape[2]
    groups = lax.axis_size("bead")
    share = atoms_here // (2 * groups)
    basis, freq, index = mode_basis()
    cosine = jnp.cos(time_step * freq)[:, None, None]
    safe = jnp.where(index == 0, 1.0, freq)
    sinc = jnp.where(index == 0, time_step, jnp.sin(time_step * freq) / safe)[:, None, None]
    wsin = (freq * jnp.sin(time_step * freq))[:, None, None]
    half = 0.5 * time_step
    aux = aux_momenta
    force = forces
    for step in range(STEPS):
        momenta = momenta + half * force
        shaped_q = positions.reshape(beads_here, 3, 2, groups * share)
        shaped_p = momenta.reshape(beads_here, 3, 2, groups * share)
        owned_q, owned_p = (
            lax.all_to_all(shaped_q, "bead", split_axis=3, concat_axis=0, tiled=True),
            lax.all_to_all(shaped_p, "bead", split_axis=3, concat_axis=0, tiled=True),
        )
        new_q, new_p, aux = mode_step(
            owned_q.reshape(BEADS, 3, 2 * share),
            owned_p.reshape(BEADS, 3, 2 * share),
            aux,
            noise[step],
            basis,
            cosine,
            sinc,
            wsin,
            gle_drift,
            gle_noise_mix,
        )
        back_q, back_p = (
            lax.all_to_all(
                new_q.reshape(BEADS, 3, 2, share), "bead", split_axis=0, concat_axis=3, tiled=True
            ),
            lax.all_to_all(
                new_p.reshape(BEADS, 3, 2, share), "bead", split_axis=0, concat_axis=3, tiled=True
            ),
        )
        positions = back_q.reshape(beads_here, 3, atoms_here)
        momenta = back_p.reshape(beads_here, 3, atoms_here)
        force = pair_forces(positions)
        momenta = momenta + half * force
    return (positions, momenta, force, aux)


def solution(mesh):
    in_specs = (
        P("bead", None, "space"),
        P("bead", None, "space"),
        P("bead", None, "space"),
        P(),
        P(),
        P(None, None, None, ("space", "bead")),
        P(None, None, None, None, ("space", "bead")),
    )
    out_specs = (
        P("bead", None, "space"),
        P("bead", None, "space"),
        P("bead", None, "space"),
        P(None, None, None, ("space", "bead")),
    )
    return jax.shard_map(
        on_device, mesh=mesh, in_specs=in_specs, out_specs=out_specs, check_vma=False
    )
```

profile of v0, /device:TPU:0, one launch (start us, length us, event | category | flops | bytes accessed | tf_op | source)
XLA Modules:
  0.0 409.9 jit_solution(560465266027311314)
XLA Ops:
  2.0 8.3 %copy.360 = f32[2,3,2,4096]{1,2,0,3:T(2,128)} copy(f32[2,3,2,4096]{3,2,0,1:T(2,128)S(1)} %reshape.141) | data formatting | bytes 393216 | tf_op jit(solution)/shard_map/reshape | solution.py:141
  10.3 14.3 %reshape.167 = f32[16,1,3072]{2,1,0:T(1,128)} reshape(f32[4096,2,2,3]{3,2,1,0:T(2,128)} %bitcast.238) | data formatting | bytes 393216
  24.6 8.3 %all-to-all-start.1 = ((f32[16,1,3072]{2,1,0:T(1,128)}), f32[16,1,3072]{2,1,0:T(1,128)S(1)}, u32[]{:S(2)}, u32[]{:S(2)}) async-start(f32[16,1,3072]{2,1,0:T(1,128)} %reshape.167), calls=%async_computation.1 | async-start | bytes 393216 | tf_op jit(solution)/shard_map/all_to_all | solution.py:144
  33.7 8.3 %copy.356 = f32[2,3,2,4096]{1,2,0,3:T(2,128)} copy(f32[2,3,2,4096]{3,2,0,1:T(2,128)S(1)} %reshape.139) | data formatting | bytes 393216 | tf_op jit(solution)/shard_map/reshape | solution.py:140
  42.0 14.2 %reshape.165 = f32[16,1,3072]{2,1,0:T(1,128)} reshape(f32[4096,2,2,3]{3,2,1,0:T(2,128)} %bitcast.239) | data formatting | bytes 393216
  57.9 7.4 %all-to-all-start = ((f32[16,1,3072]{2,1,0:T(1,128)}), f32[16,1,3072]{2,1,0:T(1,128)S(1)}, u32[]{:S(2)}, u32[]{:S(2)}) async-start(f32[16,1,3072]{2,1,0:T(1,128)} %reshape.165), calls=%async_computation | async-start | bytes 393216 | tf_op jit(solution)/shard_map/all_to_all | solution.py:143
  70.1 14.8 %reshape.168 = f32[4096,2,2,3]{3,2,1,0:T(2,128)} reshape(f32[16,3072]{1,0:T(8,128)S(1)} %reduce.1) | data formatting | bytes 393216
  84.9 6.8 %copy.423 = f32[2,3,2,16,256]{4,3,2,1,0:T(8,128)S(1)} copy(f32[2,3,2,16,256]{1,2,0,4,3:T(2,128)} %bitcast.240) | data formatting | bytes 393216 | tf_op jit(solution)/shard_map/all_to_all | solution.py:144
  93.9 14.8 %reshape.166 = f32[4096,2,2,3]{3,2,1,0:T(2,128)} reshape(f32[16,3072]{1,0:T(8,128)S(1)} %reduce) | data formatting | bytes 393216
  108.8 7.0 %copy.421 = f32[2,3,2,16,256]{4,3,2,1,0:T(8,128)S(1)} copy(f32[2,3,2,16,256]{1,2,0,4,3:T(2,128)} %bitcast.241) | data formatting | bytes 393216 | tf_op jit(solution)/shard_map/all_to_all | solution.py:143
  122.9 7.0 %all-to-all-start.2 = ((f32[32,3,2,256]{3,2,1,0:T(2,128)}), f32[32,3,2,256]{3,2,1,0:T(2,128)S(1)}, u32[]{:S(2)}, u32[]{:S(2)}) async-start(f32[32,3,2,256]{3,2,1,0:T(2,128)} %copy.370), calls=%async_computation.2 | async-start | bytes 393216 | tf_op jit(solution)/shard_map/all_to_all | solution.py:159
  130.0 8.1 %all-to-all-done.2 = f32[32,3,2,256]{3,2,1,0:T(2,128)S(1)} async-done(((f32[32,3,2,256]{3,2,1,0:T(2,128)}), f32[32,3,2,256]{3,2,1,0:T(2,128)S(1)}, u32[]{:S(2)}, u32[]{:S(2)}) %all-to-all-start.2) | async-done | bytes 196640 | tf_op jit(solution)/shard_map/all_to_all | solution.py:159
  143.6 64.1 %while.32 = (s32[]{:T(128)}, f32[2,3,65,128]{3,1,2,0:T(4,128)S(1)}, f32[2,3,65,128]{3,1,2,0:T(4,128)S(1)}, s32[]{:T(128)}, s32[]{:T(128)}, /*index=5*/s32[]{:T(128)}, s32[]{:T(128)}, s32[]{:T(128)}, f32[3]{0:T(128)S(1)}) while((s32[]{:T(128)}, f32[2,3,65,128]{3,1,2,0:T(4,128)S(1)}, f32[2,3,65,128]{3,1,2,0:T(4,128)S(1)}, ...), condition=%wide.region_6.7_spmd.clone, body=%wide.region_0.6_spmd.sunk.clone.sunk | while | flops 101412872 | bytes 11750121 | solution.py:103
  144.2 4.5 %fusion.237 = (f32[2,16,128]{2,1,0:T(8,128)S(1)}, f32[2,16,128]{2,1,0:T(8,128)S(1)}, f32[2,16,128,128]{2,3,1,0:T(8,128)S(1)}) fusion(f32[2,3,65,128]{3,1,2,0:T(4,128)S(1)} %get-tuple-element.447, s32[]{:T(128)S(6)} %select_n.174, f32[3]{0:T(128)S(1)} %get-tuple-element.453, s32[]{:T(128)S(6)} %select_n.173, ...), kind=kOutput, calls=%fused_computation.231.clone.1 | convolution fusion | flops 22548480 | bytes 2294280 | tf_op jit(solution)/shard_map/while/body/eval_jaxpr/xcni,xcnj->xnij/dot_general | solution.py:53
  160.0 4.5 %fusion.237 = (f32[2,16,128]{2,1,0:T(8,128)S(1)}, f32[2,16,128]{2,1,0:T(8,128)S(1)}, f32[2,16,128,128]{2,3,1,0:T(8,128)S(1)}) fusion(f32[2,3,65,128]{3,1,2,0:T(4,128)S(1)} %get-tuple-element.447, s32[]{:T(128)S(6)} %select_n.174, f32[3]{0:T(128)S(1)} %get-tuple-element.453, s32[]{:T(128)S(6)} %select_n.173, ...), kind=kOutput, calls=%fused_computation.231.clone.1 | convolution fusion | flops 22548480 | bytes 2294280 | tf_op jit(solution)/shard_map/while/body/eval_jaxpr/xcni,xcnj->xnij/dot_general | solution.py:53
  175.9 4.5 %fusion.237 = (f32[2,16,128]{2,1,0:T(8,128)S(1)}, f32[2,16,128]{2,1,0:T(8,128)S(1)}, f32[2,16,128,128]{2,3,1,0:T(8,128)S(1)}) fusion(f32[2,3,65,128]{3,1,2,0:T(4,128)S(1)} %get-tuple-element.447, s32[]{:T(128)S(6)} %select_n.174, f32[3]{0:T(128)S(1)} %get-tuple-element.453, s32[]{:T(128)S(6)} %select_n.173, ...), kind=kOutput, calls=%fused_computation.231.clone.1 | convolution fusion | flops 22548480 | bytes 2294280 | tf_op jit(solution)/shard_map/while/body/eval_jaxpr/xcni,xcnj->xnij/dot_general | solution.py:53
  191.8 4.5 %fusion.237 = (f32[2,16,128]{2,1,0:T(8,128)S(1)}, f32[2,16,128]{2,1,0:T(8,128)S(1)}, f32[2,16,128,128]{2,3,1,0:T(8,128)S(1)}) fusion(f32[2,3,65,128]{3,1,2,0:T(4,128)S(1)} %get-tuple-element.447, s32[]{:T(128)S(6)} %select_n.174, f32[3]{0:T(128)S(1)} %get-tuple-element.453, s32[]{:T(128)S(6)} %select_n.173, ...), kind=kOutput, calls=%fused_computation.231.clone.1 | convolution fusion | flops 22548480 | bytes 2294280 | tf_op jit(solution)/shard_map/while/body/eval_jaxpr/xcni,xcnj->xnij/dot_general | solution.py:53
  208.3 8.5 %copy.428 = f32[2,3,2,16,256]{1,2,0,4,3:T(2,128)} copy(f32[2,3,2,16,256]{4,2,1,0,3:T(2,128)S(1)} %bitcast.246) | data formatting | bytes 393216 | tf_op jit(solution)/shard_map/all_to_all | solution.py:159
  216.8 14.2 %reshape.169 = f32[16,1,3072]{2,1,0:T(1,128)} reshape(f32[4096,2,2,3]{3,2,1,0:T(2,128)} %bitcast.237) | data formatting | bytes 393216
  231.0 6.6 %all-to-all-start.3 = ((f32[16,1,3072]{2,1,0:T(1,128)}), f32[16,1,3072]{2,1,0:T(1,128)S(1)}, u32[]{:S(2)}, u32[]{:S(2)}) async-start(f32[16,1,3072]{2,1,0:T(1,128)} %reshape.169), calls=%async_computation.3 | async-start | bytes 393216 | tf_op jit(solution)/shard_map/all_to_all | solution.py:143
  238.0 8.3 %copy.384 = f32[2,3,2,4096]{1,2,0,3:T(2,128)} copy(f32[2,3,2,4096]{3,2,1,0:T(2,128)S(1)} %add_add_fusion) | data formatting | bytes 393216 | tf_op jit(solution)/shard_map/add | solution.py:139
  246.3 14.2 %reshape.171 = f32[16,1,3072]{2,1,0:T(1,128)} reshape(f32[4096,2,2,3]{3,2,1,0:T(2,128)} %bitcast.242) | data formatting | bytes 393216
  260.5 6.9 %all-to-all-start.5 = ((f32[16,1,3072]{2,1,0:T(1,128)}), f32[16,1,3072]{2,1,0:T(1,128)S(1)}, u32[]{:S(2)}, u32[]{:S(2)}) async-start(f32[16,1,3072]{2,1,0:T(1,128)} %reshape.171), calls=%async_computation.5 | async-start | bytes 393216 | tf_op jit(solution)/shard_map/all_to_all | solution.py:144
  270.5 14.8 %reshape.170 = f32[4096,2,2,3]{3,2,1,0:T(2,128)} reshape(f32[16,3072]{1,0:T(8,128)S(1)} %reduce.2) | data formatting | bytes 393216
  285.3 6.8 %copy.429 = f32[2,3,2,16,256]{4,3,2,1,0:T(8,128)S(1)} copy(f32[2,3,2,16,256]{1,2,0,4,3:T(2,128)} %bitcast.243) | data formatting | bytes 393216 | tf_op jit(solution)/shard_map/all_to_all | solution.py:143
  294.1 14.8 %reshape.172 = f32[4096,2,2,3]{3,2,1,0:T(2,128)} reshape(f32[16,3072]{1,0:T(8,128)S(1)} %reduce.3) | data formatting | bytes 393216
  308.9 7.3 %copy.433 = f32[2,3,2,16,256]{4,3,2,1,0:T(8,128)S(1)} copy(f32[2,3,2,16,256]{1,2,0,4,3:T(2,128)} %bitcast.244) | data formatting | bytes 393216 | tf_op jit(solution)/shard_map/all_to_all | solution.py:144
  321.7 6.9 %all-to-all-start.6 = ((f32[32,3,2,256]{3,2,1,0:T(2,128)}), f32[32,3,2,256]{3,2,1,0:T(2,128)S(1)}, u32[]{:S(2)}, u32[]{:S(2)}) async-start(f32[32,3,2,256]{3,2,1,0:T(2,128)} %copy.394), calls=%async_computation.6 | async-start | bytes 393216 | tf_op jit(solution)/shard_map/all_to_all | solution.py:159
  328.6 8.1 %all-to-all-done.6 = f32[32,3,2,256]{3,2,1,0:T(2,128)S(1)} async-done(((f32[32,3,2,256]{3,2,1,0:T(2,128)}), f32[32,3,2,256]{3,2,1,0:T(2,128)S(1)}, u32[]{:S(2)}, u32[]{:S(2)}) %all-to-all-start.6) | async-done | bytes 196640 | tf_op jit(solution)/shard_map/all_to_all | solution.py:159
  342.2 63.7 %while.33 = (s32[]{:T(128)}, f32[2,3,65,128]{3,1,2,0:T(4,128)S(1)}, f32[2,3,65,128]{3,1,2,0:T(4,128)S(1)}, s32[]{:T(128)}, s32[]{:T(128)}, /*index=5*/s32[]{:T(128)}, s32[]{:T(128)}, s32[]{:T(128)}, f32[3]{0:T(128)S(1)}) while((s32[]{:T(128)}, f32[2,3,65,128]{3,1,2,0:T(4,128)S(1)}, f32[2,3,65,128]{3,1,2,0:T(4,128)S(1)}, ...), condition=%wide.region_13.14_spmd.clone, body=%wide.region_7.13_spmd.sunk.clone.sunk | while | flops 101412872 | bytes 11750121 | solution.py:103
  358.4 4.5 %fusion.247 = (f32[2,16,128]{2,1,0:T(8,128)S(1)}, f32[2,16,128]{2,1,0:T(8,128)S(1)}, f32[2,16,128,128]{2,3,1,0:T(8,128)S(1)}) fusion(f32[2,3,65,128]{3,1,2,0:T(4,128)S(1)} %get-tuple-element.474, s32[]{:T(128)S(6)} %select_n.176, f32[3]{0:T(128)S(1)} %get-tuple-element.480, s32[]{:T(128)S(6)} %select_n.175, ...), kind=kOutput, calls=%fused_computation.232.clone.1 | convolution fusion | flops 22548480 | bytes 2294280 | tf_op jit(solution)/shard_map/while/body/eval_jaxpr/xcni,xcnj->xnij/dot_general | solution.py:53
  374.3 4.5 %fusion.247 = (f32[2,16,128]{2,1,0:T(8,128)S(1)}, f32[2,16,128]{2,1,0:T(8,128)S(1)}, f32[2,16,128,128]{2,3,1,0:T(8,128)S(1)}) fusion(f32[2,3,65,128]{3,1,2,0:T(4,128)S(1)} %get-tuple-element.474, s32[]{:T(128)S(6)} %select_n.176, f32[3]{0:T(128)S(1)} %get-tuple-element.480, s32[]{:T(128)S(6)} %select_n.175, ...), kind=kOutput, calls=%fused_computation.232.clone.1 | convolution fusion | flops 22548480 | bytes 2294280 | tf_op jit(solution)/shard_map/while/body/eval_jaxpr/xcni,xcnj->xnij/dot_general | solution.py:53
  (163 shorter events, 143.3 us)
Async XLA Ops:
  10.3 22.8 %copy-start.8 = (f32[32,5,5]{0,2,1:T(8,128)S(1)}, f32[32,5,5]{0,2,1:T(8,128)}, u32[]{:S(2)}) copy-start(f32[32,5,5]{0,2,1:T(8,128)} %param.16) | copy-start | bytes 9604
  10.3 23.0 %copy-start.9 = (f32[32,5,5]{0,2,1:T(8,128)S(1)}, f32[32,5,5]{0,2,1:T(8,128)}, u32[]{:S(2)}) copy-start(f32[32,5,5]{0,2,1:T(8,128)} %param.17) | copy-start | bytes 9604
  10.3 23.1 %copy-start.7 = (f32[2,3,8192]{2,0,1:T(2,128)S(1)}, f32[2,3,8192]{2,0,1:T(2,128)}, u32[]{:S(2)}) copy-start(f32[2,3,8192]{2,0,1:T(2,128)} %param.13) | copy-start | bytes 589828
  24.6 33.3 %all-to-all-start.1 = ((f32[16,1,3072]{2,1,0:T(1,128)}), f32[16,1,3072]{2,1,0:T(1,128)S(1)}, u32[]{:S(2)}, u32[]{:S(2)}) async-start(f32[16,1,3072]{2,1,0:T(1,128)} %reshape.167), calls=%async_computation.1 | async-start | bytes 393216 | tf_op jit(solution)/shard_map/all_to_all | solution.py:144
  57.9 34.9 %all-to-all-start = ((f32[16,1,3072]{2,1,0:T(1,128)}), f32[16,1,3072]{2,1,0:T(1,128)S(1)}, u32[]{:S(2)}, u32[]{:S(2)}) async-start(f32[16,1,3072]{2,1,0:T(1,128)} %reshape.165), calls=%async_computation | async-start | bytes 393216 | tf_op jit(solution)/shard_map/all_to_all | solution.py:143
  115.8 3.7 copy-start
  120.6 1.0 copy-start.1
  122.1 16.2 %copy-start.2 = (f32[32,5,3,512]{3,0,2,1:T(8,128)S(1)}, f32[32,5,3,512]{3,0,2,1:T(8,128)}, u32[]{:S(2)}) copy-start(f32[32,5,3,512]{3,0,2,1:T(8,128)} %copy-done.1) | copy-start | bytes 2949124
  122.9 15.1 %all-to-all-start.2 = ((f32[32,3,2,256]{3,2,1,0:T(2,128)}), f32[32,3,2,256]{3,2,1,0:T(2,128)S(1)}, u32[]{:S(2)}, u32[]{:S(2)}) async-start(f32[32,3,2,256]{3,2,1,0:T(2,128)} %copy.370), calls=%async_computation.2 | async-start | bytes 393216 | tf_op jit(solution)/shard_map/all_to_all | solution.py:159
  130.0 13.6 %copy-start.6 = (f32[3]{0:T(128)S(1)}, f32[3]{0:T(128)}, u32[]{:S(2)}) copy-start(f32[3]{0:T(128)} %constant.208.clone..sunk.4) | copy-start | bytes 40
  138.2 4.9 %collective-permute-start = (f32[2,3,128]{2,0,1:T(2,128)S(1)}, f32[2,3,128]{2,0,1:T(2,128)S(1)}, u32[]{:S(2)}, u32[]{:S(2)}) collective-permute-start(f32[2,3,128]{2,0,1:T(2,128)S(1)} %slice.57), channel_id=1, source_target_pairs={{1,0},{0,1},{3,2},{2,3},{5,4},{4,5},{7,6},{6,7},{9,8},{8,9},{11,10... | collective-permute-start | bytes 9224 | tf_op jit(solution)/shard_map/ppermute | solution.py:23
  139.6 77.2 %all-to-all-start.4 = ((f32[32,3,2,256]{3,2,1,0:T(2,128)}), f32[32,3,2,256]{3,2,1,0:T(2,128)S(1)}, u32[]{:S(2)}, u32[]{:S(2)}) async-start(f32[32,3,2,256]{3,2,1,0:T(2,128)} %copy.376), calls=%async_computation.4 | async-start | bytes 393216 | tf_op jit(solution)/shard_map/all_to_all | solution.py:162
  207.7 30.0 %collective-permute-start.1 = (f32[2,3,128]{2,1,0:T(4,128)S(1)}, f32[2,3,128]{2,1,0:T(4,128)S(1)}, u32[]{:S(2)}, u32[]{:S(2)}) collective-permute-start(f32[2,3,128]{2,1,0:T(4,128)S(1)} %slice_bitcast_fusion.9), channel_id=1, source_target_pairs={{1,0},{0,1},{3,2},{2,3},{5,4},{4,5},{7,6},{6,7},{9,8},{8,9},{11,10... | collective-permute-start | bytes 9224 | tf_op jit(solution)/shard_map/ppermute | solution.py:23
  231.0 29.5 %all-to-all-start.3 = ((f32[16,1,3072]{2,1,0:T(1,128)}), f32[16,1,3072]{2,1,0:T(1,128)S(1)}, u32[]{:S(2)}, u32[]{:S(2)}) async-start(f32[16,1,3072]{2,1,0:T(1,128)} %reshape.169), calls=%async_computation.3 | async-start | bytes 393216 | tf_op jit(solution)/shard_map/all_to_all | solution.py:143
  260.5 32.5 %all-to-all-start.5 = ((f32[16,1,3072]{2,1,0:T(1,128)}), f32[16,1,3072]{2,1,0:T(1,128)S(1)}, u32[]{:S(2)}, u32[]{:S(2)}) async-start(f32[16,1,3072]{2,1,0:T(1,128)} %reshape.171), calls=%async_computation.5 | async-start | bytes 393216 | tf_op jit(solution)/shard_map/all_to_all | solution.py:144
  308.9 8.2 %slice-start = ((f32[32,5,3,512]{3,0,2,1:T(8,128)}), f32[32,4,3,512]{3,0,2,1:T(8,128)S(1)}, s32[]{:S(2)}) async-start(f32[32,5,3,512]{3,0,2,1:T(8,128)} %copy-done.1), calls=%async_computation.8 | async-start | bytes 1572864 | tf_op jit(solution)/shard_map/slice | solution.py:122
  320.3 17.9 %copy-start.3 = (f32[32,5,3,512]{3,0,2,1:T(8,128)}, f32[32,5,3,512]{3,0,2,1:T(8,128)S(1)}, u32[]{:S(2)}) copy-start(f32[32,5,3,512]{3,0,2,1:T(8,128)S(1)} %bitcast_add_fusion) | copy-start | bytes 2949124
  321.7 15.0 %all-to-all-start.6 = ((f32[32,3,2,256]{3,2,1,0:T(2,128)}), f32[32,3,2,256]{3,2,1,0:T(2,128)S(1)}, u32[]{:S(2)}, u32[]{:S(2)}) async-start(f32[32,3,2,256]{3,2,1,0:T(2,128)} %copy.394), calls=%async_computation.6 | async-start | bytes 393216 | tf_op jit(solution)/shard_map/all_to_all | solution.py:159
  336.8 5.4 %copy-start.4 = (f32[2,3,8192]{2,0,1:T(2,128)}, f32[2,3,8192]{2,0,1:T(2,128)S(1)}, u32[]{:S(2)}) copy-start(f32[2,3,8192]{2,0,1:T(2,128)S(1)} %reshape.151) | copy-start | bytes 589828
  336.9 4.9 %collective-permute-start.2 = (f32[2,3,128]{2,0,1:T(2,128)S(1)}, f32[2,3,128]{2,0,1:T(2,128)S(1)}, u32[]{:S(2)}, u32[]{:S(2)}) collective-permute-start(f32[2,3,128]{2,0,1:T(2,128)S(1)} %slice.62), channel_id=1, source_target_pairs={{1,0},{0,1},{3,2},{2,3},{5,4},{4,5},{7,6},{6,7},{9,8},{8,9},{11,10... | collective-permute-start | bytes 9224 | tf_op jit(solution)/shard_map/ppermute | solution.py:23
  338.2 70.2 %all-to-all-start.7 = ((f32[32,3,2,256]{3,2,1,0:T(2,128)}), f32[32,3,2,256]{3,2,1,0:T(2,128)S(1)}, u32[]{:S(2)}, u32[]{:S(2)}) async-start(f32[32,3,2,256]{3,2,1,0:T(2,128)} %copy.396), calls=%async_computation.7 | async-start | bytes 393216 | tf_op jit(solution)/shard_map/all_to_all | solution.py:162
  405.9 1.1 slice-start.1
  405.9 2.8 collective-permute-start.3
  408.9 0.8 copy-start.5
where the time goes:
time: 416 us; the launch traced here: 410 us
  local copies, waits for them, and re-layouts  190 us (46%)
  matrix products  140 us (34%)
  starting transfers between devices  51.4 us (12%)
  waiting for transfers between devices  16.2 us (4%)
  other arithmetic  10.1 us (2%)
    unnamed x33, local copies, waits for them, and re-layouts  119 us
    dot_general x16, matrix products, tile_weight(): jnp.einsum('xcni,xcnj->xnij', center, other, precision=lax.Precision.HIGH...  68.3 us
    dot_general x8, matrix products, mutual(): jnp.einsum('xnij,xcni->xcnj', weight, center, precision=lax.Precision.HIG...  27.2 us
    all_to_all x2, waiting for transfers between devices, on_device(): lax.all_to_all(new_q.reshape(BEADS, 3, 2, share), 'bead', split_axis=0, c...  16.2 us
    all_to_all x2, starting transfers between devices, on_device(): lax.all_to_all(shaped_p, 'bead', split_axis=3, concat_axis=0, tiled=True)  15.2 us
    dot_general x8, matrix products, pull(): jnp.einsum('xnij,xcnj->xcni', weight, other, precision=lax.Precision.HIGH...  15.2 us
    dot_general x8, matrix products, mutual(): jnp.einsum('xnij,xcnj->xcni', weight, other, precision=lax.Precision.HIGH...  15.2 us
    all_to_all x5, local copies, waits for them, and re-layouts, on_device(): lax.all_to_all(shaped_q, 'bead', split_axis=3, concat_axis=0, tiled=True)  14.7 us
  transfers between devices with their start and end apart: 12, of which 2 were waited for; matrix products, arithmetic and copies ran while one was open for 62% of the time, Pallas kernels for 0%

commit v1 on v0

v1 whole, which is shorter than its diff:
```python
import functools
import math

import jax
import jax.numpy as jnp
import ml_dtypes
import numpy as np
from jax import lax
from jax.experimental import pallas as pl
from jax.experimental.pallas import tpu as pltpu
from jax.sharding import PartitionSpec as P

CELL_ATOMS = 128
AUX = 4
STEPS = 2

time_step = 0.5
cycle_freq = 1.5
cell_length = 2.0
pair_strength = 0.1
pair_range = 1.0

LANES = 128
LOG2E = math.log2(math.e)
HIGHEST = lax.Precision.HIGHEST
VMEM_SPEC = pl.BlockSpec(memory_space=pltpu.VMEM)
SMEM_SPEC = pl.BlockSpec(memory_space=pltpu.SMEM)


def call(kernel, out_shape, in_specs=None, scratch_shapes=(), **kwargs):
    many = isinstance(out_shape, (list, tuple))
    return pl.pallas_call(
        kernel,
        out_shape=out_shape,
        in_specs=in_specs,
        out_specs=[VMEM_SPEC] * len(out_shape) if many else VMEM_SPEC,
        scratch_shapes=scratch_shapes,
        compiler_params=pltpu.CompilerParams(vmem_limit_bytes=56 * 1024 * 1024),
        **kwargs,
    )


def f32(*shape):
    return jax.ShapeDtypeStruct(shape, jnp.float32)


def mode_tables(beads):
    j = np.arange(beads, dtype=np.float64)[:, None]
    k = np.arange(beads)[None, :]
    phase = 2.0 * np.pi * j * k / beads
    basis = np.where(
        k == 0,
        np.sqrt(1.0 / beads),
        np.where(
            k < beads // 2,
            np.sqrt(2.0 / beads) * np.cos(phase),
            np.where(
                k == beads // 2, np.sqrt(1.0 / beads) * np.cos(phase), np.sqrt(2.0 / beads) * np.sin(phase)
            ),
        ),
    )
    freq = 2.0 * cycle_freq * np.sin(np.pi * np.arange(beads) / beads)
    cosine = np.cos(time_step * freq)
    safe = np.where(np.arange(beads) == 0, 1.0, freq)
    sinc = np.where(np.arange(beads) == 0, time_step, np.sin(time_step * freq) / safe)
    wsin = freq * np.sin(time_step * freq)
    turn = np.stack([cosine, sinc, wsin], axis=1)
    return basis.astype(np.float32), turn.astype(np.float32)


def split3(value):
    first = value.astype(jnp.bfloat16).astype(jnp.float32)
    rest = value - first
    second = rest.astype(jnp.bfloat16).astype(jnp.float32)
    third = rest - second
    return first, second, third


def run_force(coords):
    width = coords.shape[1]
    inner = width // CELL_ATOMS - 2
    row = lax.broadcasted_iota(jnp.int32, (8, width), 0)
    coords = jnp.where(row < 3, coords, 0.0)

    def half_square(x):
        return (0.5 * LOG2E / pair_range) * jnp.sum(x * x, axis=0, keepdims=True)

    left = jnp.where(row < 3, coords * (LOG2E / pair_range), 0.0)
    left = jnp.where(row == 3, -half_square(coords), left)
    left = jnp.where(row == 4, 1.0, left)
    a1, a2, a3 = split3(left)
    left = jnp.transpose(jnp.concatenate([a1, a1, a2, a2, a1, a3], axis=0)).astype(jnp.bfloat16)

    def right(shift):
        x = jnp.where(row == 0, coords + shift, coords)
        x = jnp.where(row == 4, -half_square(x), x)
        x = jnp.where(row == 3, 1.0, x)
        b1, b2, b3 = split3(x)
        return jnp.concatenate([b1, b2, b1, b2, b3, b1], axis=0).astype(jnp.bfloat16)

    rights = {delta: right(delta * cell_length) for delta in (-1, 0, 1)}

    def cell(array, number, axis):
        return lax.slice_in_dim(array, number * CELL_ATOMS, (number + 1) * CELL_ATOMS, axis=axis)

    forces = []
    for number in range(1, inner + 1):
        total = jnp.zeros((16, CELL_ATOMS), jnp.float32)
        for delta in (-1, 0, 1):
            power = jnp.dot(
                cell(left, number + delta, 0),
                cell(rights[-delta], number, 1),
                preferred_element_type=jnp.float32,
            )
            weight = jnp.exp2(power)
            high = weight.astype(jnp.bfloat16)
            low = (weight - high.astype(jnp.float32)).astype(jnp.bfloat16)
            rows = cell(rights[delta], number + delta, 1)[:16]
            total = total + jnp.dot(rows, high, preferred_element_type=jnp.float32)
            total = total + jnp.dot(rows, low, preferred_element_type=jnp.float32)
        total = total[:8] + total[8:]
        center = cell(coords, number, 1)
        forces.append(
            (pair_strength / pair_range) * (center * total[3:4] - total)
        )
    return jnp.concatenate(forces, axis=1)


def send_kernel(q_ref, p_ref, f_ref, out_ref, *, groups, span):
    beads_here = q_ref.shape[0]
    half = q_ref.shape[2] // 2
    rows = beads_here * 2 * span * 3
    quarter = 0.5 * time_step

    def one(b, carry):
        for j in range(beads_here):
            for h in range(2):
                for u in range(span):
                    at = pl.multiple_of(h * half + (b * span + u) * LANES, LANES)
                    place = ((j * 2 + h) * span + u) * 3
                    lanes = pl.ds(at, LANES)
                    out_ref[pl.ds(b * 2 * rows + place, 3), :] = q_ref[j, :, lanes]
                    out_ref[pl.ds(b * 2 * rows + rows + place, 3), :] = (
                        p_ref[j, :, lanes] + quarter * f_ref[j, :, lanes]
                    )
        return carry

    lax.fori_loop(0, groups, one, 0)


def noise_kernel(drift_ref, mix_ref, aux_ref, noise_ref, first_ref, second_ref):
    beads = aux_ref.shape[0]
    size = AUX + 1
    tiles = aux_ref.shape[3] // LANES

    def one(k, carry):
        base = k * size * size
        noises = [noise_ref[0, k, b] for b in range(size)]
        others = [aux_ref[k, b] for b in range(AUX)]
        for a in range(size):
            total = mix_ref[base + a * size] * noises[0]
            for b in range(1, size):
                total = total + mix_ref[base + a * size + b] * noises[b]
            for b in range(AUX):
                total = total + drift_ref[base + a * size + b + 1] * others[b]
            for t in range(tiles):
                first_ref[a, t, pl.ds(k * 3, 3), :] = total[:, t * LANES : (t + 1) * LANES]
        noises = [noise_ref[1, k, b] for b in range(size)]
        for a in range(size):
            total = mix_ref[base + a * size] * noises[0]
            for b in range(1, size):
                total = total + mix_ref[base + a * size + b] * noises[b]
            for t in range(tiles):
                second_ref[a, t, pl.ds(k * 3, 3), :] = total[:, t * LANES : (t + 1) * LANES]
        return carry

    lax.fori_loop(0, beads, one, 0)


def strided(ref, start, size, stride):
    return ref[pl.ds(start, size, stride=stride), :]


def turned(qm, p0, turn):
    cosine, sinc, wsin = turn[:, 0:1], turn[:, 1:2], turn[:, 2:3]
    return qm * cosine + sinc * p0, p0 * cosine - wsin * qm


def first_kernel(
    flag_ref, got_ref, pre_ref, gather_ref, basis_ref, turn_ref, drift_ref,
    own_ref, up0_ref, up1_ref, dn0_ref, dn1_ref, qn_ref, pn_ref, aux_ref, *, groups, span,
):
    beads = basis_ref.shape[0]
    beads_here = beads // groups
    rows = beads_here * 2 * span * 3
    places = [(h, u, c) for h in range(2) for u in range(span) for c in range(3)]

    def gathered(which):
        columns = []
        for h, u, c in places:
            parts = [
                strided(got_ref, which * rows + ((j * 2 + h) * span + u) * 3 + c, groups, 2 * rows)
                for j in range(beads_here)
            ]
            columns.append(jnp.concatenate(parts, axis=0))
        return jnp.concatenate(columns, axis=1)

    gather = gather_ref[...]
    qm = jnp.dot(gather, gathered(0), precision=HIGHEST, preferred_element_type=jnp.float32)
    pm = jnp.dot(gather, gathered(1), precision=HIGHEST, preferred_element_type=jnp.float32)

    def pre(a):
        return jnp.concatenate(
            [strided(pre_ref.at[a, h * span + u], c, beads, 3) for h, u, c in places], axis=1
        )

    drift = drift_ref[...]
    p0 = drift[:, 0:1] * pm + pre(0)
    for a in range(1, AUX + 1):
        aux_ref[a - 1] = drift[:, a * (AUX + 1) : a * (AUX + 1) + 1] * pm + pre(a)
    qn, pn = turned(qm, p0, turn_ref[...])
    qn_ref[...] = qn
    pn_ref[...] = pn
    new = jnp.dot(basis_ref[...], qn, precision=HIGHEST, preferred_element_type=jnp.float32)
    own_ref[...] = jnp.zeros_like(own_ref)
    value = {}
    for number, (h, u, c) in enumerate(places):
        value[h, u, c] = new[:, number * LANES : (number + 1) * LANES]
        own_ref[h, u, pl.ds(c, beads, stride=8), :] = value[h, u, c]
    top = flag_ref[0] == groups - 1
    bottom = flag_ref[0] == 0
    for c in range(3):
        here = pl.ds(c * beads, beads)
        last0, last1 = value[0, span - 1, c], value[1, span - 1, c]
        up0_ref[here, :] = jnp.where(top, last1, last0)
        up1_ref[here, :] = jnp.where(top, last0, last1)
        dn0_ref[here, :] = jnp.where(bottom, value[1, 0, c], value[0, 0, c])
        dn1_ref[here, :] = jnp.where(bottom, value[0, 0, c], value[1, 0, c])


def second_kernel(
    own_ref, up0_ref, up1_ref, dn0_ref, dn1_ref, qn_ref, pn_ref, aux_ref, pre_ref,
    spread_ref, basis_ref, turn_ref, drift_ref,
    sendq_ref, sendp_ref, auxout_ref, halo_ref, force_ref, *, span,
):
    beads = basis_ref.shape[0]
    places = [(h, u, c) for h in range(2) for u in range(span) for c in range(3)]
    halo_ref[...] = jnp.zeros_like(halo_ref)
    for number, ref in enumerate((up0_ref, up1_ref, dn0_ref, dn1_ref)):
        for c in range(3):
            halo_ref[number, pl.ds(c, beads, stride=8), :] = ref[pl.ds(c * beads, beads), :]

    def one(bead, carry):
        here = pl.ds(pl.multiple_of(bead * 8, 8), 8)
        for h in range(2):
            coords = jnp.concatenate(
                [halo_ref[h, here, :]]
                + [own_ref[h, u, here, :] for u in range(span)]
                + [halo_ref[2 + h, here, :]],
                axis=1,
            )
            force = run_force(coords)
            for u in range(span):
                force_ref[h, u, here, :] = force[:, u * LANES : (u + 1) * LANES]
        return carry

    lax.fori_loop(0, beads, one, 0)

    force = jnp.concatenate([strided(force_ref.at[h, u], c, beads, 8) for h, u, c in places], axis=1)
    fm = jnp.dot(spread_ref[...], force, precision=HIGHEST, preferred_element_type=jnp.float32)
    pm = pn_ref[...] + time_step * fm
    drift = drift_ref[...]
    state = [pm] + [aux_ref[a] for a in range(AUX)]
    news = []
    for a in range(AUX + 1):
        total = jnp.concatenate(
            [strided(pre_ref.at[a, h * span + u], c, beads, 3) for h, u, c in places], axis=1
        )
        for b in range(AUX + 1):
            number = a * (AUX + 1) + b
            total = total + drift[:, number : number + 1] * state[b]
        news.append(total)
    for a in range(AUX):
        auxout_ref[a] = news[a + 1]
    qn, pn = turned(qn_ref[...], news[0], turn_ref[...])
    basis = basis_ref[...]
    newq = jnp.dot(basis, qn, precision=HIGHEST, preferred_element_type=jnp.float32)
    newp = jnp.dot(basis, pn, precision=HIGHEST, preferred_element_type=jnp.float32)
    for number in range(len(places)):
        lanes = slice(number * LANES, (number + 1) * LANES)
        sendq_ref[pl.ds(number, beads, stride=len(places)), :] = newq[:, lanes]
        sendp_ref[pl.ds(number, beads, stride=len(places)), :] = newp[:, lanes]


def aux_kernel(aux_ref, out_ref, rows_ref):
    beads = aux_ref.shape[1]
    tiles = out_ref.shape[3] // LANES
    for a in range(AUX):
        for t in range(tiles):
            for c in range(3):
                number = t * 3 + c
                rows_ref[a * tiles + t, pl.ds(c, beads, stride=3), :] = aux_ref[
                    a, :, number * LANES : (number + 1) * LANES
                ]

    def one(k, carry):
        for a in range(AUX):
            for t in range(tiles):
                out_ref[k, a, :, t * LANES : (t + 1) * LANES] = rows_ref[a * tiles + t, pl.ds(k * 3, 3), :]
        return carry

    lax.fori_loop(0, beads, one, 0)


def bead_kernel(got_ref, before_ref, after_ref, q_ref, f_ref, x_ref, *, groups, span, block):
    beads_here = q_ref.shape[0]
    cells = q_ref.shape[2] // LANES
    x_ref[...] = jnp.zeros_like(x_ref)
    for j in range(beads_here):
        x_ref[j, 0:3, 0:LANES] = before_ref[j]
        x_ref[j, 0:3, (cells + 1) * LANES : (cells + 2) * LANES] = after_ref[j]

    def place(b, carry):
        for j in range(beads_here):
            for h in range(2):
                for u in range(span):
                    row = b * (beads_here * 2 * span * 3) + ((j * 2 + h) * span + u) * 3
                    cell = h * (cells // 2) + b * span + u
                    value = got_ref[pl.ds(row, 3), :]
                    q_ref[j, :, pl.ds(pl.multiple_of(cell * LANES, LANES), LANES)] = value
                    x_ref[j, 0:3, pl.ds(pl.multiple_of((cell + 1) * LANES, LANES), LANES)] = value
        return carry

    lax.fori_loop(0, groups, place, 0)

    def one(number, carry):
        at = pl.multiple_of(number * block * LANES, LANES)
        for j in range(beads_here):
            force = run_force(x_ref[j, :, pl.ds(at, (block + 2) * LANES)])
            f_ref[j, :, pl.ds(at, block * LANES)] = force[0:3]
        return carry

    lax.fori_loop(0, cells // block, one, 0)


def last_kernel(got_ref, f_ref, out_ref, *, groups, span):
    beads_here = f_ref.shape[0]
    cells = f_ref.shape[2] // LANES
    half = 0.5 * time_step

    def place(b, carry):
        for j in range(beads_here):
            for h in range(2):
                for u in range(span):
                    row = b * (beads_here * 2 * span * 3) + ((j * 2 + h) * span + u) * 3
                    cell = h * (cells // 2) + b * span + u
                    lanes = pl.ds(pl.multiple_of(cell * LANES, LANES), LANES)
                    out_ref[j, :, lanes] = got_ref[pl.ds(row, 3), :] + half * f_ref[j, :, lanes]
        return carry

    lax.fori_loop(0, groups, place, 0)


def on_device(positions, momenta, forces, gle_drift, gle_noise_mix, aux_momenta, noise):
    beads_here, _, atoms_here = positions.shape
    beads = gle_drift.shape[0]
    groups = lax.axis_size("bead")
    spaces = lax.axis_size("space")
    share = atoms_here // (2 * groups)
    span = share // CELL_ATOMS
    cells = atoms_here // CELL_ATOMS
    columns = 2 * span * 3
    width = columns * LANES
    size = AUX + 1
    basis, turn = mode_tables(beads)
    order = np.array([b * beads_here + j for j in range(beads_here) for b in range(groups)])
    gather = jnp.asarray(np.ascontiguousarray(basis[order].T))
    spread = jnp.asarray(np.ascontiguousarray(basis.T))
    basis = jnp.asarray(basis)
    turn = jnp.asarray(turn)
    drift_rows = gle_drift.reshape(beads, size * size)
    me = lax.axis_index("bead").astype(jnp.int32).reshape(1)

    def exchanged(block):
        return lax.all_to_all(block, "bead", split_axis=0, concat_axis=0, tiled=True)

    send = call(
        functools.partial(send_kernel, groups=groups, span=span),
        f32(groups * 2 * beads_here * columns, LANES),
        [VMEM_SPEC] * 3,
    )(positions, momenta, forces)
    got = exchanged(send)
    first, second = call(
        noise_kernel,
        [f32(size, 2 * span, beads * 3, LANES)] * 2,
        [SMEM_SPEC, SMEM_SPEC, VMEM_SPEC, VMEM_SPEC],
    )(gle_drift.reshape(-1), gle_noise_mix.reshape(-1), aux_momenta, noise)

    halo = f32(beads * 3, LANES)
    own, up0, up1, dn0, dn1, qn, pn, aux = call(
        functools.partial(first_kernel, groups=groups, span=span),
        [f32(2, span, beads * 8, LANES), halo, halo, halo, halo, f32(beads, width), f32(beads, width),
         f32(AUX, beads, width)],
        [SMEM_SPEC] + [VMEM_SPEC] * 6,
    )(me, got, first, gather, basis, turn, drift_rows)

    def shifted(block, step, wrap):
        route = []
        for b in range(groups):
            for s in range(spaces):
                to_b, to_s = b + step, s
                if not 0 <= to_b < groups:
                    to_b, to_s = to_b % groups, (s + wrap) % spaces
                route.append((b * spaces + s, to_b * spaces + to_s))
        return lax.ppermute(block, ("bead", "space"), route)

    up0 = shifted(up0, 1, 1)
    up1 = shifted(up1, 1, 0)
    dn0 = shifted(dn0, -1, 0)
    dn1 = shifted(dn1, -1, -1)

    rows = beads * columns
    sendq, sendp, aux = call(
        functools.partial(second_kernel, span=span),
        [f32(rows, LANES), f32(rows, LANES), f32(AUX, beads, width)],
        [VMEM_SPEC] * 13,
        scratch_shapes=[
            pltpu.VMEM((4, beads * 8, LANES), jnp.float32),
            pltpu.VMEM((2, span, beads * 8, LANES), jnp.float32),
        ],
    )(own, up0, up1, dn0, dn1, qn, pn, aux, second, spread, basis, turn, drift_rows)
    gotq = exchanged(sendq)
    gotp = exchanged(sendp)
    aux_out = call(
        aux_kernel,
        f32(*aux_momenta.shape),
        [VMEM_SPEC],
        scratch_shapes=[pltpu.VMEM((AUX * 2 * span, beads * 3, LANES), jnp.float32)],
    )(aux)

    per_owner = gotq.reshape(groups, beads_here, 2 * span, 3, LANES)
    head = per_owner[0, :, 0]
    tail = per_owner[groups - 1, :, 2 * span - 1]
    before = lax.ppermute(tail, "space", [(s, (s + 1) % spaces) for s in range(spaces)])
    after = lax.ppermute(head, "space", [(s, (s - 1) % spaces) for s in range(spaces)])
    block = math.gcd(cells, 8)
    positions_out, forces_out = call(
        functools.partial(bead_kernel, groups=groups, span=span, block=block),
        [f32(*positions.shape)] * 2,
        [VMEM_SPEC] * 3,
        scratch_shapes=[pltpu.VMEM((beads_here, 8, (cells + 2) * LANES), jnp.float32)],
    )(gotq, before, after)
    momenta_out = call(
        functools.partial(last_kernel, groups=groups, span=span),
        f32(*momenta.shape),
        [VMEM_SPEC] * 2,
    )(gotp, forces_out)
    return positions_out, momenta_out, forces_out, aux_out


def solution(mesh):
    in_specs = (
        P("bead", None, "space"),
        P("bead", None, "space"),
        P("bead", None, "space"),
        P(),
        P(),
        P(None, None, None, ("space", "bead")),
        P(None, None, None, None, ("space", "bead")),
    )
    out_specs = (
        P("bead", None, "space"),
        P("bead", None, "space"),
        P("bead", None, "space"),
        P(None, None, None, ("space", "bead")),
    )
    return jax.shard_map(
        on_device, mesh=mesh, in_specs=in_specs, out_specs=out_specs, check_vma=False
    )
```

time: 416 us -> 141 us (0.34); the launches traced: 410 us -> 140 us
  local copies, waits for them, and re-layouts: 190 us -> 22.7 us
  matrix products: 140 us -> 0 us
  Pallas kernels: 0 us -> 78.4 us
  starting transfers between devices: 51.4 us -> 19.5 us
  blocking collectives: 0 us -> 14.2 us
  waiting for transfers between devices: 16.2 us -> 4.93 us
  other arithmetic: 10.1 us -> 0 us
    dot_general x52 -> x0, matrix products: 140 us -> none  [the longest x16 68.3 us: tile_weight(): jnp.einsum('xcni,xcnj->xnij', center, other, precision=lax.Precision.HIGH...]
    unnamed x33 -> x39, local copies, waits for them, and re-layouts: 119 us -> 20.4 us
    pallas_call x0 -> x7, Pallas kernels: none -> 78.4 us  [the longest x1 35.5 us: on_device(): call(functools.partial(second_kernel, span=span), [f32(rows, LANES), f32(...]
    all_to_all x8 -> x2, starting transfers between devices: 50.2 us -> 12 us  [exchanged(): lax.all_to_all(block, 'bead', split_axis=0, concat_axis=0, tiled=True)]
    all_to_all x13 -> x1, local copies, waits for them, and re-layouts: 37.7 us -> 0.04 us  [exchanged(): lax.all_to_all(block, 'bead', split_axis=0, concat_axis=0, tiled=True)]
    reshape x23 -> x4, local copies, waits for them, and re-layouts: 21.9 us -> 2.27 us  [the longest x1 0.8 us: on_device(): gle_noise_mix.reshape(-1)]
    all_to_all x8 -> x2, waiting for transfers between devices: 16.2 us -> 0.63 us  [exchanged(): lax.all_to_all(block, 'bead', split_axis=0, concat_axis=0, tiled=True)]
    all_to_all x0 -> x1, blocking collectives: none -> 14.2 us  [exchanged(): lax.all_to_all(block, 'bead', split_axis=0, concat_axis=0, tiled=True)]
  transfers between devices with their start and end apart: 12 -> 8, of which waited for: 2 -> 4; matrix products, arithmetic and copies ran while one was open for 62% -> 8% of each run, Pallas kernels for 0% -> 25%
where the time goes in v1:
time: 141 us; the launch traced here: 140 us
  Pallas kernels  78.4 us (56%)
  local copies, waits for them, and re-layouts  22.7 us (16%)
  starting transfers between devices  19.5 us (14%)
  blocking collectives  14.2 us (10%)
  waiting for transfers between devices  4.93 us (3%)
    pallas_call x1, Pallas kernels, on_device(): call(functools.partial(second_kernel, span=span), [f32(rows, LANES), f32(...  35.5 us
    pallas_call x1, Pallas kernels, on_device(): call(functools.partial(bead_kernel, groups=groups, span=span, block=block...  28 us
    unnamed x39, local copies, waits for them, and re-layouts  20.4 us
    all_to_all x1, blocking collectives, exchanged(): lax.all_to_all(block, 'bead', split_axis=0, concat_axis=0, tiled=True)  14.2 us
    all_to_all x2, starting transfers between devices, exchanged(): lax.all_to_all(block, 'bead', split_axis=0, concat_axis=0, tiled=True)  12 us
    ppermute x4, starting transfers between devices, shifted(): return lax.ppermute(block, ('bead', 'space'), route)  6.96 us
    pallas_call x1, Pallas kernels, on_device(): call(noise_kernel, [f32(size, 2 * span, beads * 3, LANES)] * 2, [SMEM_SPE...  5.13 us
    ppermute x4, waiting for transfers between devices, shifted(): return lax.ppermute(block, ('bead', 'space'), route)  4.29 us
  transfers between devices with their start and end apart: 8, of which 4 were waited for; matrix products, arithmetic and copies ran while one was open for 8% of the time, Pallas kernels for 25%

profile of v1, /device:TPU:0, one launch (start us, length us, event | category | flops | bytes accessed | tf_op | source)
XLA Modules:
  0.0 140.4 jit_solution(7660243370956381264)
XLA Ops:
  0.7 1.9 %copy.42.q_ref = f32[2,3,8192]{2,1,0:T(4,128)} copy(f32[2,3,8192]{2,0,1:T(2,128)} %param.11) | data formatting | bytes 393216 | tf_op args[0]
  2.6 1.8 %copy.43.p_ref = f32[2,3,8192]{2,1,0:T(4,128)} copy(f32[2,3,8192]{2,0,1:T(2,128)} %param.12) | data formatting | bytes 393216 | tf_op args[1]
  4.3 1.8 %copy.44.f_ref = f32[2,3,8192]{2,1,0:T(4,128)} copy(f32[2,3,8192]{2,0,1:T(2,128)} %param.13) | data formatting | bytes 393216 | tf_op args[2]
  6.1 2.1 %shard_map.138 = f32[768,128]{1,0:T(8,128)} custom-call(f32[2,3,8192]{2,1,0:T(4,128)} %copy.42.q_ref, f32[2,3,8192]{2,1,0:T(4,128)} %copy.43.p_ref, f32[2,3,8192]{2,1,0:T(4,128)} %copy.44.f_ref), custom_call_target="tpu_custom_call" | custom-call | tf_op jit(solution)/shard_map/pallas_call | solution.py:387
  8.2 8.5 %all-to-all-start = ((f32[16,48,128]{2,1,0:T(8,128)}), f32[16,48,128]{2,1,0:T(8,128)S(1)}, u32[]{:S(2)}, u32[]{:S(2)}) async-start(f32[16,48,128]{2,1,0:T(8,128)} %bitcast.18), calls=%async_computation | async-start | bytes 786432 | tf_op jit(solution)/shard_map/all_to_all | solution.py:385
  16.9 2.9 %copy.48.noise_ref = f32[2,32,5,3,512]{4,3,2,1,0:T(4,128)} copy(f32[2,32,5,3,512]{4,1,3,2,0:T(8,128)S(1)} %copy-done) | data formatting | bytes 3932160 | tf_op args[6]
  19.8 1.4 copy.47.aux_ref
  21.1 0.8 reshape.31.drift_ref
  22.1 0.8 reshape.32.mix_ref
  22.9 0.7 copy.49.drift_ref
  23.6 5.1 %shard_map.139 = (f32[5,4,96,128]{3,2,1,0:T(8,128)}, f32[5,4,96,128]{3,2,1,0:T(8,128)}) custom-call(f32[800]{0:T(1024)} %reshape.31.drift_ref, f32[800]{0:T(1024)} %reshape.32.mix_ref, f32[32,4,3,512]{3,2,1,0:T(4,128)} %copy.47.aux_ref, f32[2,32,5,3,512]{4,3,2,1,0:T(4,128)} %copy.48.noise_ref), custom_call_target="tpu_custom_call" | custom-call | tf_op jit(solution)/shard_map/pallas_call | solution.py:393
  28.7 0.6 all-to-all-done
  29.3 0.8 copy-done.2
  30.1 3.1 %shard_map.140 = (f32[2,2,256,128]{3,2,1,0:T(8,128)}, f32[96,128]{1,0:T(8,128)}, f32[96,128]{1,0:T(8,128)}, f32[96,128]{1,0:T(8,128)}, f32[96,128]{1,0:T(8,128)}...) custom-call(s32[1]{0:T(128)} %bitcast.flag_ref, f32[768,128]{1,0:T(8,128)} %bitcast.17, ...), custom_call_target="tpu_custom_call" | custom-call | tf_op jit(solution)/shard_map/pallas_call | solution.py:400
  33.2 1.3 collective-permute-start
  34.5 1.5 %collective-permute-start.1 = (f32[96,128]{1,0:T(8,128)}, f32[96,128]{1,0:T(8,128)S(1)}, u32[]{:S(2)}, u32[]{:S(2)}) collective-permute-start(f32[96,128]{1,0:T(8,128)} %get-tuple-element.22), channel_id=1, source_target_pairs={{0,2},{1,3},{2,4},{3,5},{4,6},{5,7},{6,8},{7,9},{8,10},{9,11},{10,... | collective-permute-start | bytes 147464 | tf_op jit(solution)/shard_map/ppermute | solution.py:415
  36.0 4.2 %collective-permute-start.2 = (f32[96,128]{1,0:T(8,128)}, f32[96,128]{1,0:T(8,128)S(1)}, u32[]{:S(2)}, u32[]{:S(2)}) collective-permute-start(f32[96,128]{1,0:T(8,128)} %get-tuple-element.23), channel_id=1, source_target_pairs={{0,30},{1,31},{2,0},{3,1},{4,2},{5,3},{6,4},{7,5},{8,6},{9,7},{10,... | collective-permute-start | bytes 147464 | tf_op jit(solution)/shard_map/ppermute | solution.py:415
  40.1 0.9 collective-permute-done.up0_ref
  41.0 1.4 collective-permute-done.1.up1_ref
  42.4 2.0 %collective-permute-done.3.dn1_ref = f32[96,128]{1,0:T(8,128)S(1)} collective-permute-done((f32[96,128]{1,0:T(8,128)}, f32[96,128]{1,0:T(8,128)S(1)}, u32[]{:S(2)}, u32[]{:S(2)}) %collective-permute-start.3) | collective-permute-done | bytes 49184 | tf_op jit(solution)/shard_map/ppermute | solution.py:415
  44.5 0.6 copy-done.9
  45.1 35.5 %shard_map.141 = (f32[384,128]{1,0:T(8,128)}, f32[384,128]{1,0:T(8,128)}, f32[4,32,1536]{2,1,0:T(8,128)}) custom-call(f32[2,2,256,128]{3,2,1,0:T(8,128)} %get-tuple-element.20.own_ref, f32[96,128]{1,0:T(8,128)} %copy-done.6, f32[96,128]{1,0:T(8,128)} %copy-done.7, f32[96,128]{1,0:T(8,128)} %copy-done.8, f32[96,128]{1,0:T(8,128)} %copy-done.9, ...), custom_call_target="tpu_custom_call" | custom-call | tf_op jit(solution)/shard_map/pallas_call | solution.py:423
  80.6 14.2 %all_to_all.33 = f32[16,24,128]{2,1,0:T(8,128)S(1)} all-to-all(f32[16,24,128]{2,1,0:T(8,128)} %bitcast.22), channel_id=1, replica_groups=mesh['bead'=16,'space'=2] {'bead'}, dimensions={0} | all-to-all | bytes 393216 | tf_op jit(solution)/shard_map/all_to_all | solution.py:385
  94.7 3.5 %all-to-all-start.2 = ((f32[16,24,128]{2,1,0:T(8,128)}), f32[16,24,128]{2,1,0:T(8,128)S(1)}, u32[]{:S(2)}, u32[]{:S(2)}) async-start(f32[16,24,128]{2,1,0:T(8,128)} %bitcast.21), calls=%async_computation.2 | async-start | bytes 393216 | tf_op jit(solution)/shard_map/all_to_all | solution.py:385
  98.9 2.6 %shard_map.144 = f32[32,4,3,512]{3,2,1,0:T(4,128)} custom-call(f32[4,32,1536]{2,1,0:T(8,128)} %get-tuple-element.33.aux_ref), custom_call_target="tpu_custom_call" | custom-call | tf_op jit(solution)/shard_map/pallas_call | solution.py:434
  101.5 2.4 %copy.57 = f32[32,4,3,512]{3,1,2,0:T(4,128)} copy(f32[32,4,3,512]{3,2,1,0:T(4,128)} %shard_map.144) | data formatting | bytes 1572864
  104.5 28.0 %shard_map.142 = (f32[2,3,8192]{2,1,0:T(4,128)}, f32[2,3,8192]{2,1,0:T(4,128)}) custom-call(f32[384,128]{1,0:T(8,128)} %bitcast.16, f32[2,3,128]{2,1,0:T(4,128)} %copy-done.11, f32[2,3,128]{2,1,0:T(4,128)} %copy-done.12), custom_call_target="tpu_custom_call" | custom-call | tf_op jit(solution)/shard_map/pallas_call | solution.py:447
  132.5 1.8 %copy.56 = f32[2,3,8192]{2,0,1:T(2,128)} copy(f32[2,3,8192]{2,1,0:T(4,128)} %get-tuple-element.44.f_ref) | data formatting | bytes 393216
  134.3 0.7 copy-done.4
  134.9 1.9 %shard_map.143 = f32[2,3,8192]{2,1,0:T(4,128)} custom-call(f32[384,128]{1,0:T(8,128)} %bitcast.19, f32[2,3,8192]{2,1,0:T(4,128)} %get-tuple-element.44.f_ref), custom_call_target="tpu_custom_call" | custom-call | tf_op jit(solution)/shard_map/pallas_call | solution.py:453
  136.9 1.8 %copy.55 = f32[2,3,8192]{2,0,1:T(2,128)} copy(f32[2,3,8192]{2,1,0:T(4,128)} %shard_map.143) | data formatting | bytes 393216
  138.7 1.8 %copy.54 = f32[2,3,8192]{2,0,1:T(2,128)} copy(f32[2,3,8192]{2,1,0:T(4,128)} %get-tuple-element.42) | data formatting | bytes 393216
  (37 shorter events, 1.5 us)
Async XLA Ops:
  0.6 16.1 %copy-start.5 = (f32[32,5,5]{0,2,1:T(8,128)S(1)}, f32[32,5,5]{0,2,1:T(8,128)}, u32[]{:S(2)}) copy-start(f32[32,5,5]{0,2,1:T(8,128)} %param.14) | copy-start | bytes 9604
  0.6 16.2 %copy-start = (f32[2,32,5,3,512]{4,1,3,2,0:T(8,128)S(1)}, f32[2,32,5,3,512]{4,1,3,2,0:T(8,128)}, u32[]{:S(2)}) copy-start(f32[2,32,5,3,512]{4,1,3,2,0:T(8,128)} %param.17) | copy-start | bytes 5898244
  8.2 11.5 %copy-start.3 = (f32[32,4,3,512]{3,1,2,0:T(4,128)S(1)}, f32[32,4,3,512]{3,1,2,0:T(4,128)}, u32[]{:S(2)}) copy-start(f32[32,4,3,512]{3,1,2,0:T(4,128)} %param.16) | copy-start | bytes 2359300
  8.2 21.1 %all-to-all-start = ((f32[16,48,128]{2,1,0:T(8,128)}), f32[16,48,128]{2,1,0:T(8,128)S(1)}, u32[]{:S(2)}, u32[]{:S(2)}) async-start(f32[16,48,128]{2,1,0:T(8,128)} %bitcast.18), calls=%async_computation | async-start | bytes 786432 | tf_op jit(solution)/shard_map/all_to_all | solution.py:385
  16.9 5.1 %copy-start.10 = (f32[32,5,5]{0,2,1:T(8,128)S(1)}, f32[32,5,5]{0,2,1:T(8,128)}, u32[]{:S(2)}) copy-start(f32[32,5,5]{0,2,1:T(8,128)} %param.15) | copy-start | bytes 9604
  29.3 0.8 copy-start.2
  33.2 7.9 %collective-permute-start = (f32[96,128]{1,0:T(8,128)}, f32[96,128]{1,0:T(8,128)S(1)}, u32[]{:S(2)}, u32[]{:S(2)}) collective-permute-start(f32[96,128]{1,0:T(8,128)} %get-tuple-element.21), channel_id=1, source_target_pairs={{0,2},{1,3},{2,4},{3,5},{4,6},{5,7},{6,8},{7,9},{8,10},{9,11},{10,... | collective-permute-start | bytes 147464 | tf_op jit(solution)/shard_map/ppermute | solution.py:415
  34.5 7.9 %collective-permute-start.1 = (f32[96,128]{1,0:T(8,128)}, f32[96,128]{1,0:T(8,128)S(1)}, u32[]{:S(2)}, u32[]{:S(2)}) collective-permute-start(f32[96,128]{1,0:T(8,128)} %get-tuple-element.22), channel_id=1, source_target_pairs={{0,2},{1,3},{2,4},{3,5},{4,6},{5,7},{6,8},{7,9},{8,10},{9,11},{10,... | collective-permute-start | bytes 147464 | tf_op jit(solution)/shard_map/ppermute | solution.py:415
  36.0 6.4 %collective-permute-start.2 = (f32[96,128]{1,0:T(8,128)}, f32[96,128]{1,0:T(8,128)S(1)}, u32[]{:S(2)}, u32[]{:S(2)}) collective-permute-start(f32[96,128]{1,0:T(8,128)} %get-tuple-element.23), channel_id=1, source_target_pairs={{0,30},{1,31},{2,0},{3,1},{4,2},{5,3},{6,4},{7,5},{8,6},{9,7},{10,... | collective-permute-start | bytes 147464 | tf_op jit(solution)/shard_map/ppermute | solution.py:415
  40.1 4.3 %collective-permute-start.3 = (f32[96,128]{1,0:T(8,128)}, f32[96,128]{1,0:T(8,128)S(1)}, u32[]{:S(2)}, u32[]{:S(2)}) collective-permute-start(f32[96,128]{1,0:T(8,128)} %get-tuple-element.24), channel_id=1, source_target_pairs={{0,31},{1,30},{2,0},{3,1},{4,2},{5,3},{6,4},{7,5},{8,6},{9,7},{10,... | collective-permute-start | bytes 147464 | tf_op jit(solution)/shard_map/ppermute | solution.py:415
  41.0 3.4 %copy-start.6 = (f32[96,128]{1,0:T(8,128)}, f32[96,128]{1,0:T(8,128)S(1)}, u32[]{:S(2)}) copy-start(f32[96,128]{1,0:T(8,128)S(1)} %collective-permute-done.up0_ref) | copy-start | bytes 147460
  42.4 2.0 %copy-start.7 = (f32[96,128]{1,0:T(8,128)}, f32[96,128]{1,0:T(8,128)S(1)}, u32[]{:S(2)}) copy-start(f32[96,128]{1,0:T(8,128)S(1)} %collective-permute-done.1.up1_ref) | copy-start | bytes 147460
  42.4 2.0 %copy-start.8 = (f32[96,128]{1,0:T(8,128)}, f32[96,128]{1,0:T(8,128)S(1)}, u32[]{:S(2)}) copy-start(f32[96,128]{1,0:T(8,128)S(1)} %collective-permute-done.2.dn0_ref) | copy-start | bytes 147460
  44.4 0.6 copy-start.9
  94.7 9.2 %copy-start.1 = (f32[16,24,128]{2,1,0:T(8,128)}, f32[16,24,128]{2,1,0:T(8,128)S(1)}, u32[]{:S(2)}) copy-start(f32[16,24,128]{2,1,0:T(8,128)S(1)} %all_to_all.33) | copy-start | bytes 589828
  94.7 39.5 %all-to-all-start.2 = ((f32[16,24,128]{2,1,0:T(8,128)}), f32[16,24,128]{2,1,0:T(8,128)S(1)}, u32[]{:S(2)}, u32[]{:S(2)}) async-start(f32[16,24,128]{2,1,0:T(8,128)} %bitcast.21), calls=%async_computation.2 | async-start | bytes 393216 | tf_op jit(solution)/shard_map/all_to_all | solution.py:385
  98.3 5.6 %collective-permute-start.4 = (f32[2,3,128]{2,1,0:T(4,128)S(1)}, f32[2,3,128]{2,1,0:T(4,128)S(1)}, u32[]{:S(2)}, u32[]{:S(2)}) collective-permute-start(f32[2,3,128]{2,1,0:T(4,128)S(1)} %bitcast.23), channel_id=1, source_target_pairs={{0,1},{1,0},{2,3},{3,2},{4,5},{5,4},{6,7},{7,6},{8,9},{9,8},{10,11... | collective-permute-start | bytes 9224 | tf_op jit(solution)/shard_map/ppermute | solution.py:444
  98.4 5.5 %collective-permute-start.5 = (f32[2,3,128]{2,1,0:T(4,128)S(1)}, f32[2,3,128]{2,1,0:T(4,128)S(1)}, u32[]{:S(2)}, u32[]{:S(2)}) collective-permute-start(f32[2,3,128]{2,1,0:T(4,128)S(1)} %bitcast.24), channel_id=1, source_target_pairs={{0,1},{1,0},{2,3},{3,2},{4,5},{5,4},{6,7},{7,6},{8,9},{9,8},{10,11... | collective-permute-start | bytes 9224 | tf_op jit(solution)/shard_map/ppermute | solution.py:445
  103.9 0.6 copy-start.11
  103.9 0.6 copy-start.12
  134.3 0.7 copy-start.4

commit v2 on v1

v2 whole, which is shorter than its diff:
```python
import functools
import math

import jax
import jax.numpy as jnp
import ml_dtypes
import numpy as np
from jax import lax
from jax.experimental import pallas as pl
from jax.experimental.pallas import tpu as pltpu
from jax.sharding import PartitionSpec as P

CELL_ATOMS = 128
AUX = 4
STEPS = 2

time_step = 0.5
cycle_freq = 1.5
cell_length = 2.0
pair_strength = 0.1
pair_range = 1.0

LANES = 128
LOG2E = math.log2(math.e)
HIGHEST = lax.Precision.HIGHEST
VMEM_SPEC = pl.BlockSpec(memory_space=pltpu.VMEM)
SMEM_SPEC = pl.BlockSpec(memory_space=pltpu.SMEM)


def call(kernel, out_shape, in_specs=None, scratch_shapes=(), **kwargs):
    many = isinstance(out_shape, (list, tuple))
    return pl.pallas_call(
        kernel,
        out_shape=out_shape,
        in_specs=in_specs,
        out_specs=[VMEM_SPEC] * len(out_shape) if many else VMEM_SPEC,
        scratch_shapes=scratch_shapes,
        compiler_params=pltpu.CompilerParams(vmem_limit_bytes=56 * 1024 * 1024),
        **kwargs,
    )


def f32(*shape):
    return jax.ShapeDtypeStruct(shape, jnp.float32)


def mode_tables(beads):
    j = np.arange(beads, dtype=np.float64)[:, None]
    k = np.arange(beads)[None, :]
    phase = 2.0 * np.pi * j * k / beads
    basis = np.where(
        k == 0,
        np.sqrt(1.0 / beads),
        np.where(
            k < beads // 2,
            np.sqrt(2.0 / beads) * np.cos(phase),
            np.where(
                k == beads // 2, np.sqrt(1.0 / beads) * np.cos(phase), np.sqrt(2.0 / beads) * np.sin(phase)
            ),
        ),
    )
    freq = 2.0 * cycle_freq * np.sin(np.pi * np.arange(beads) / beads)
    cosine = np.cos(time_step * freq)
    safe = np.where(np.arange(beads) == 0, 1.0, freq)
    sinc = np.where(np.arange(beads) == 0, time_step, np.sin(time_step * freq) / safe)
    wsin = freq * np.sin(time_step * freq)
    turn = np.stack([cosine, sinc, wsin], axis=1)
    return basis.astype(np.float32), turn.astype(np.float32)


def split3(value):
    first = value.astype(jnp.bfloat16).astype(jnp.float32)
    rest = value - first
    second = rest.astype(jnp.bfloat16).astype(jnp.float32)
    third = rest - second
    return first, second, third


def prepare(coords, left_ref, right_ref, slot, want_left, shifts):
    row = lax.broadcasted_iota(jnp.int32, coords.shape, 0)

    def half_square(x):
        return (0.5 * LOG2E / pair_range) * jnp.sum(x * x, axis=0, keepdims=True)

    if want_left:
        x = jnp.where(row == 3, -half_square(coords), coords * (LOG2E / pair_range))
        x = jnp.where(row == 4, 1.0, x)
        a1, a2, a3 = split3(x)
        left = jnp.concatenate([a1, a1, a2, a2, a1, a3], axis=0)
        left_ref[slot] = jnp.transpose(left).astype(jnp.bfloat16)
    for delta in shifts:
        x = jnp.where(row == 0, coords + delta * cell_length, coords) if delta else coords
        x = jnp.where(row == 4, -half_square(x), x)
        x = jnp.where(row == 3, 1.0, x)
        b1, b2, b3 = split3(x)
        right_ref[slot, delta + 1] = jnp.concatenate([b1, b2, b1, b2, b3, b1], axis=0).astype(jnp.bfloat16)


def pair_scratch(slots, tiles):
    count = sum(len(of) for of in tiles)
    return [
        pltpu.VMEM((slots, CELL_ATOMS, 48), jnp.bfloat16),
        pltpu.VMEM((slots, 3, 48, CELL_ATOMS), jnp.bfloat16),
        pltpu.VMEM((count * CELL_ATOMS, CELL_ATOMS), jnp.float32),
        pltpu.VMEM((count * CELL_ATOMS, CELL_ATOMS), jnp.float32),
        pltpu.VMEM((2 * count * CELL_ATOMS, CELL_ATOMS), jnp.bfloat16),
        pltpu.VMEM((2 * count * CELL_ATOMS, CELL_ATOMS), jnp.bfloat16),
    ]


def pair_sums(steps, tiles, base_of, finish, left_ref, right_ref, e0_ref, e1_ref, w0_ref, w1_ref):
    n = CELL_ATOMS

    def powers(step, e_ref):
        base = base_of(step)
        at = 0
        for u, of in enumerate(tiles):
            for offset, delta in of:
                e_ref[at * n : (at + 1) * n] = jnp.dot(
                    left_ref[base + offset],
                    right_ref[base + 1 + u, 1 - delta],
                    preferred_element_type=jnp.float32,
                )
                at += 1

    def weights(e_ref, w_ref):
        at = 0
        for of in tiles:
            for number in range(len(of)):
                weight = jnp.exp2(e_ref[(at + number) * n : (at + number + 1) * n])
                high = weight.astype(jnp.bfloat16)
                low = (weight - high.astype(jnp.float32)).astype(jnp.bfloat16)
                place = 2 * at + number
                w_ref[place * n : (place + 1) * n] = high
                place += len(of)
                w_ref[place * n : (place + 1) * n] = low
            at += len(of)

    def sums(step, w_ref):
        base = base_of(step)
        at = 0
        for u, of in enumerate(tiles):
            if not of:
                continue
            rows = [right_ref[base + offset, delta + 1, 0:16] for offset, delta in of]
            total = jnp.dot(
                jnp.concatenate(rows + rows, axis=1),
                w_ref[2 * at * n : 2 * (at + len(of)) * n],
                preferred_element_type=jnp.float32,
            )
            finish(step, u, total[:8] + total[8:])
            at += len(of)

    def clamp(step):
        return jnp.clip(step, 0, steps - 1)

    def pair(i, carry):
        step = 2 * i
        sums(clamp(step - 2), w0_ref)
        weights(e1_ref, w1_ref)
        powers(clamp(step), e0_ref)
        sums(clamp(step - 1), w1_ref)
        weights(e0_ref, w0_ref)
        powers(clamp(step + 1), e1_ref)
        return carry

    lax.fori_loop(0, (steps + 3) // 2, pair, 0)


def place_loop(groups, span, one):
    def body(b, carry):
        for h in range(2):
            for u in range(span):
                cell = (h * groups + b) * span + u
                one(b, h * span + u, cell)
        return carry

    lax.fori_loop(0, groups, body, 0)


def lanes_of(cell):
    return pl.ds(pl.multiple_of(cell * LANES, LANES), LANES)


def send_kernel(q_ref, p_ref, f_ref, out_ref, *, groups, span):
    here = q_ref.shape[1]
    rows = here * 2 * span * 3
    quarter = 0.5 * time_step

    def one(b, tile, cell):
        lanes = lanes_of(cell)
        for c in range(3):
            row = b * 2 * rows + (tile * 3 + c) * here
            out_ref[pl.ds(row, here), :] = q_ref[c, :, lanes]
            out_ref[pl.ds(row + rows, here), :] = p_ref[c, :, lanes] + quarter * f_ref[c, :, lanes]

    place_loop(groups, span, one)


def columns_of(tiles):
    return [(t, c, slice((t * 3 + c) * LANES, (t * 3 + c + 1) * LANES)) for t in range(tiles) for c in range(3)]


def noise_kernel(drift_ref, mix_ref, aux_ref, noise_ref, first_ref, second_ref, rows_ref):
    beads = aux_ref.shape[0]
    size = AUX + 1
    tiles = aux_ref.shape[3] // LANES

    def copy(k, carry):
        for c in range(3):
            for t in range(tiles):
                rows_ref[c, t, pl.ds(k * AUX, AUX), :] = aux_ref[k, c, :, t * LANES : (t + 1) * LANES]
        return carry

    lax.fori_loop(0, beads, copy, 0)
    drift = drift_ref[...]
    mix = mix_ref[...]
    for t, c, lanes in columns_of(tiles):
        inner = slice(t * LANES, (t + 1) * LANES)
        others = [rows_ref[c, t, pl.ds(b, beads, stride=AUX), :] for b in range(AUX)]
        for s, ref in ((0, first_ref), (1, second_ref)):
            noises = [noise_ref[s, b, c, :, inner] for b in range(size)]
            for a in range(size):
                at = a * size
                total = mix[:, at : at + 1] * noises[0]
                for b in range(1, size):
                    total = total + mix[:, at + b : at + b + 1] * noises[b]
                if s == 0:
                    for b in range(AUX):
                        total = total + drift[:, at + b + 1 : at + b + 2] * others[b]
                ref[a, :, lanes] = total


def strided(ref, start, size, stride):
    return ref[pl.ds(start, size, stride=stride), :]


def turned(qm, p0, turn):
    cosine, sinc, wsin = turn[:, 0:1], turn[:, 1:2], turn[:, 2:3]
    return qm * cosine + sinc * p0, p0 * cosine - wsin * qm


def dot(a, b):
    return jnp.dot(a, b, precision=HIGHEST, preferred_element_type=jnp.float32)


def first_kernel(
    flag_ref, got_ref, pre_ref, gather_ref, basis_ref, turn_ref, drift_ref,
    own_ref, up0_ref, up1_ref, dn0_ref, dn1_ref, qn_ref, pn_ref, pm_ref, *, groups, span,
):
    beads = basis_ref.shape[0]
    here = beads // groups
    tiles = 2 * span
    rows = here * tiles * 3

    def gathered(which):
        columns = []
        for number in range(tiles * 3):
            parts = [
                strided(got_ref, which * rows + number * here + j, groups, 2 * rows) for j in range(here)
            ]
            columns.append(jnp.concatenate(parts, axis=0))
        return jnp.concatenate(columns, axis=1)

    gather = gather_ref[...]
    qm = dot(gather, gathered(0))
    pm = dot(gather, gathered(1))
    p0 = drift_ref[:, 0:1] * pm + pre_ref[0]
    qn, pn = turned(qm, p0, turn_ref[...])
    new = dot(basis_ref[...], qn)
    own_ref[...] = jnp.zeros_like(own_ref)
    value = {}
    for t, c, lanes in columns_of(tiles):
        value[t // span, t % span, c] = new[:, lanes]
        own_ref[t // span, t % span, pl.ds(c, beads, stride=8), :] = new[:, lanes]
    top = flag_ref[0] == groups - 1
    bottom = flag_ref[0] == 0
    for c in range(3):
        part = pl.ds(c * beads, beads)
        last0, last1 = value[0, span - 1, c], value[1, span - 1, c]
        up0_ref[part, :] = jnp.where(top, last1, last0)
        up1_ref[part, :] = jnp.where(top, last0, last1)
        dn0_ref[part, :] = jnp.where(bottom, value[1, 0, c], value[0, 0, c])
        dn1_ref[part, :] = jnp.where(bottom, value[0, 0, c], value[1, 0, c])
    qn_ref[...] = qn
    pn_ref[...] = pn
    pm_ref[...] = pm


def middle_kernel(pm_ref, first_ref, second_ref, drift_ref, out_ref):
    size = AUX + 1
    drift = drift_ref[...]
    for at in range(0, pm_ref.shape[1], LANES):
        lanes = slice(at, at + LANES)
        pm = pm_ref[:, lanes]
        aux = [drift[:, a * size : a * size + 1] * pm + first_ref[a, :, lanes] for a in range(1, size)]
        for a in range(size):
            total = second_ref[a, :, lanes]
            for b in range(AUX):
                total = total + drift[:, a * size + b + 1 : a * size + b + 2] * aux[b]
            out_ref[a, :, lanes] = total


def coefficient(center, sums):
    return (pair_strength / pair_range) * (center * sums[3:4] - sums)


def inner_kernel(own_ref, force_ref, *scratch, span, tiles):
    beads = own_ref.shape[2] // 8
    left_ref, right_ref = scratch[:2]

    def tile(bead):
        return pl.ds(pl.multiple_of(bead * 8, 8), 8)

    def one(bead, carry):
        for h in range(2):
            for u in range(span):
                prepare(
                    own_ref[h, u, tile(bead), :], left_ref, right_ref,
                    (2 * bead + h) * (span + 2) + u + 1, True, (-1, 0, 1),
                )
        return carry

    lax.fori_loop(0, beads, one, 0)

    def finish(step, u, sums):
        h, here = step % 2, tile(step // 2)
        force_ref[h, u, here, :] = coefficient(own_ref[h, u, here, :], sums)

    pair_sums(2 * beads, tiles, lambda step: step * (span + 2), finish, *scratch)


def outer_kernel(
    own_ref, part_ref, up0_ref, up1_ref, dn0_ref, dn1_ref, qn_ref, pn_ref, base_ref,
    gather_ref, basis_ref, turn_ref, drift_ref,
    sendq_ref, pm_ref, p0_ref, halo_ref, force_ref, *scratch, groups, span, tiles,
):
    beads = basis_ref.shape[0]
    here = beads // groups
    left_ref, right_ref = scratch[:2]
    halo_ref[...] = jnp.zeros_like(halo_ref)
    for number, ref in enumerate((up0_ref, up1_ref, dn0_ref, dn1_ref)):
        for c in range(3):
            halo_ref[number, pl.ds(c, beads, stride=8), :] = ref[pl.ds(c * beads, beads), :]

    def tile(bead):
        return pl.ds(pl.multiple_of(bead * 8, 8), 8)

    def one(bead, carry):
        at = tile(bead)
        for h in range(2):
            slot = (2 * bead + h) * (span + 2)
            prepare(halo_ref[h, at, :], left_ref, right_ref, slot, True, (-1,))
            prepare(halo_ref[2 + h, at, :], left_ref, right_ref, slot + span + 1, True, (1,))
            for u in sorted({0, span - 1}):
                shifts = tuple(sorted(-delta for _, delta in tiles[u]))
                prepare(own_ref[h, u, at, :], left_ref, right_ref, slot + u + 1, False, shifts)
        return carry

    lax.fori_loop(0, beads, one, 0)
    force_ref[...] = part_ref[...]

    def finish(step, u, sums):
        h, at = step % 2, tile(step // 2)
        force_ref[h, u, at, :] = part_ref[h, u, at, :] + coefficient(own_ref[h, u, at, :], sums)

    pair_sums(2 * beads, tiles, lambda step: step * (span + 2), finish, *scratch)

    force = jnp.concatenate(
        [strided(force_ref.at[t // span, t % span], c, beads, 8) for t, c, _ in columns_of(2 * span)], axis=1
    )
    pm = pn_ref[...] + time_step * dot(gather_ref[...], force)
    p0 = drift_ref[:, 0:1] * pm + base_ref[0]
    qn, _ = turned(qn_ref[...], p0, turn_ref[...])
    new = dot(basis_ref[...], qn)
    count = 6 * span
    for number in range(count):
        for j in range(here):
            sendq_ref[pl.ds(number * here + j, groups, stride=count * here), :] = new[
                j * groups : (j + 1) * groups, number * LANES : (number + 1) * LANES
            ]
    pm_ref[...] = pm
    p0_ref[...] = p0


def rest_kernel(
    pm_ref, p0_ref, qn_ref, base_ref, basis_ref, turn_ref, drift_ref,
    sendp_ref, out_ref, rows_ref, *, groups, span,
):
    beads = basis_ref.shape[0]
    here = beads // groups
    size = AUX + 1
    _, pn = turned(qn_ref[...], p0_ref[...], turn_ref[...])
    new = dot(basis_ref[...], pn)
    count = 6 * span
    for number in range(count):
        for j in range(here):
            sendp_ref[pl.ds(number * here + j, groups, stride=count * here), :] = new[
                j * groups : (j + 1) * groups, number * LANES : (number + 1) * LANES
            ]
    drift = drift_ref[...]
    for t, c, lanes in columns_of(2 * span):
        pm = pm_ref[:, lanes]
        for a in range(AUX):
            at = (a + 1) * size
            rows_ref[c, t, pl.ds(a, beads, stride=AUX), :] = drift[:, at : at + 1] * pm + base_ref[a + 1, :, lanes]

    def copy(k, carry):
        for c in range(3):
            for t in range(2 * span):
                out_ref[k, c, :, t * LANES : (t + 1) * LANES] = rows_ref[c, t, pl.ds(k * AUX, AUX), :]
        return carry

    lax.fori_loop(0, beads, copy, 0)


def bead_kernel(got_ref, before_ref, after_ref, q_ref, f_ref, x_ref, force_ref, *scratch, groups, span, block, tiles):
    here = q_ref.shape[1]
    cells = q_ref.shape[2] // LANES
    left_ref, right_ref = scratch[:2]
    x_ref[...] = jnp.zeros_like(x_ref)
    for j in range(here):
        x_ref[j * (cells + 2), 0:3] = strided(before_ref, j, 3, here)
        x_ref[(j + 1) * (cells + 2) - 1, 0:3] = strided(after_ref, j, 3, here)

    def place(b, tile, cell):
        row = (b * 2 * span + tile) * 3 * here
        for c in range(3):
            q_ref[c, :, lanes_of(cell)] = got_ref[pl.ds(row + c * here, here), :]
        for j in range(here):
            x_ref[j * (cells + 2) + cell + 1, 0:3] = got_ref[pl.ds(row + j, 3, stride=here), :]

    place_loop(groups, span, place)
    slots = here * (cells + 2)
    group = math.gcd(slots, 4)

    def one(number, carry):
        for k in range(group):
            slot = number * group + k
            prepare(x_ref[slot], left_ref, right_ref, slot, True, (-1, 0, 1))
        return carry

    lax.fori_loop(0, slots // group, one, 0)
    per_bead = cells // block

    def base_of(step):
        return (step // per_bead) * (cells + 2) + (step % per_bead) * block

    def finish(step, u, sums):
        at = pl.multiple_of((step * block + u) * 8, 8)
        force_ref[pl.ds(at, 8), :] = coefficient(x_ref[base_of(step) + 1 + u], sums)

    pair_sums(here * per_bead, tiles, base_of, finish, *scratch)

    def out(cell, carry):
        for c in range(3):
            f_ref[c, :, lanes_of(cell)] = strided(force_ref, cell * 8 + c, here, cells * 8)
        return carry

    lax.fori_loop(0, cells, out, 0)


def last_kernel(got_ref, f_ref, out_ref, *, groups, span):
    here = f_ref.shape[1]
    half = 0.5 * time_step

    def one(b, tile, cell):
        lanes = lanes_of(cell)
        row = (b * 2 * span + tile) * 3 * here
        for c in range(3):
            out_ref[c, :, lanes] = got_ref[pl.ds(row + c * here, here), :] + half * f_ref[c, :, lanes]

    place_loop(groups, span, one)


def on_device(positions, momenta, forces, gle_drift, gle_noise_mix, aux_momenta, noise):
    here, _, atoms_here = positions.shape
    beads = gle_drift.shape[0]
    groups = lax.axis_size("bead")
    spaces = lax.axis_size("space")
    span = atoms_here // (2 * groups * CELL_ATOMS)
    cells = atoms_here // CELL_ATOMS
    columns = 2 * span * 3
    width = columns * LANES
    size = AUX + 1
    basis, turn = mode_tables(beads)
    order = np.array([b * here + j for j in range(here) for b in range(groups)])
    gather = jnp.asarray(np.ascontiguousarray(basis[order].T))
    basis = jnp.asarray(np.ascontiguousarray(basis[order]))
    turn = jnp.asarray(turn)
    drift = gle_drift.reshape(beads, size * size)
    mix = gle_noise_mix.reshape(beads, size * size)
    me = lax.axis_index("bead").astype(jnp.int32).reshape(1)
    by_coord = functools.partial(jnp.transpose, axes=(1, 0, 2))
    grid = f32(3, here, atoms_here)

    def exchanged(block):
        return lax.all_to_all(block, "bead", split_axis=0, concat_axis=0, tiled=True)

    send = call(
        functools.partial(send_kernel, groups=groups, span=span),
        f32(groups * 2 * here * columns, LANES),
        [VMEM_SPEC] * 3,
    )(by_coord(positions), by_coord(momenta), by_coord(forces))
    got = exchanged(send)
    rows = pltpu.VMEM((3, 2 * span, beads * AUX, LANES), jnp.float32)
    first, second = call(
        noise_kernel,
        [f32(size, beads, width)] * 2,
        [VMEM_SPEC] * 4,
        scratch_shapes=[rows],
    )(drift, mix, jnp.transpose(aux_momenta, (0, 2, 1, 3)), jnp.transpose(noise, (0, 2, 3, 1, 4)))

    halo = f32(beads * 3, LANES)
    state = f32(beads, width)
    own, up0, up1, dn0, dn1, qn, pn, pm = call(
        functools.partial(first_kernel, groups=groups, span=span),
        [f32(2, span, beads * 8, LANES), halo, halo, halo, halo, state, state, state],
        [SMEM_SPEC] + [VMEM_SPEC] * 6,
    )(me, got, first, gather, basis, turn, drift)

    def shifted(block, step, wrap):
        route = []
        for b in range(groups):
            for s in range(spaces):
                to_b, to_s = b + step, s
                if not 0 <= to_b < groups:
                    to_b, to_s = to_b % groups, (s + wrap) % spaces
                route.append((b * spaces + s, to_b * spaces + to_s))
        return lax.ppermute(block, ("bead", "space"), route)

    up0 = shifted(up0, 1, 1)
    up1 = shifted(up1, 1, 0)
    dn0 = shifted(dn0, -1, 0)
    dn1 = shifted(dn1, -1, -1)

    slots = 2 * beads * (span + 2)
    inside = [
        [(v + 1, v - u) for v in range(span) if abs(v - u) <= 1] for u in range(span)
    ]
    outside = [
        ([(0, -1)] if u == 0 else []) + ([(span + 1, 1)] if u == span - 1 else []) for u in range(span)
    ]
    part = call(
        functools.partial(inner_kernel, span=span, tiles=inside),
        f32(2, span, beads * 8, LANES),
        [VMEM_SPEC],
        scratch_shapes=pair_scratch(slots, inside),
    )(own)
    base = call(middle_kernel, f32(size, beads, width), [VMEM_SPEC] * 4)(pm, first, second, drift)
    sendq, pm, p0 = call(
        functools.partial(outer_kernel, groups=groups, span=span, tiles=outside),
        [f32(beads * columns, LANES), state, state],
        [VMEM_SPEC] * 13,
        scratch_shapes=[
            pltpu.VMEM((4, beads * 8, LANES), jnp.float32),
            pltpu.VMEM((2, span, beads * 8, LANES), jnp.float32),
        ]
        + pair_scratch(slots, outside),
    )(own, part, up0, up1, dn0, dn1, qn, pn, base, gather, basis, turn, drift)
    gotq = exchanged(sendq)
    sendp, aux_out = call(
        functools.partial(rest_kernel, groups=groups, span=span),
        [f32(beads * columns, LANES), f32(beads, 3, AUX, aux_momenta.shape[3])],
        [VMEM_SPEC] * 7,
        scratch_shapes=[rows],
    )(pm, p0, qn, base, basis, turn, drift)
    gotp = exchanged(sendp)

    head = gotq[: 3 * here]
    tail = gotq[-3 * here :]
    before = lax.ppermute(tail, "space", [(s, (s + 1) % spaces) for s in range(spaces)])
    after = lax.ppermute(head, "space", [(s, (s - 1) % spaces) for s in range(spaces)])
    block = math.gcd(cells, 2)
    around = [[(u, -1), (u + 1, 0), (u + 2, 1)] for u in range(block)]
    new_q, new_f = call(
        functools.partial(bead_kernel, groups=groups, span=span, block=block, tiles=around),
        [grid] * 2,
        [VMEM_SPEC] * 3,
        scratch_shapes=[
            pltpu.VMEM((here * (cells + 2), 8, LANES), jnp.float32),
            pltpu.VMEM((here * cells * 8, LANES), jnp.float32),
        ]
        + pair_scratch(here * (cells + 2), around),
    )(gotq, before, after)
    new_p = call(
        functools.partial(last_kernel, groups=groups, span=span),
        grid,
        [VMEM_SPEC] * 2,
    )(gotp, new_f)
    return by_coord(new_q), by_coord(new_p), by_coord(new_f), jnp.transpose(aux_out, (0, 2, 1, 3))


def solution(mesh):
    in_specs = (
        P("bead", None, "space"),
        P("bead", None, "space"),
        P("bead", None, "space"),
        P(),
        P(),
        P(None, None, None, ("space", "bead")),
        P(None, None, None, None, ("space", "bead")),
    )
    out_specs = (
        P("bead", None, "space"),
        P("bead", None, "space"),
        P("bead", None, "space"),
        P(None, None, None, ("space", "bead")),
    )
    return jax.shard_map(
        on_device, mesh=mesh, in_specs=in_specs, out_specs=out_specs, check_vma=False
    )
```

time: 141 us -> 109 us (0.77)
  local copies, waits for them, and re-layouts: 22.7 us -> 5.9 us
  blocking collectives: 14.2 us -> 0 us
  Pallas kernels: 78.4 us -> 66.9 us
  waiting for transfers between devices: 4.93 us -> 11.8 us
  starting transfers between devices: 19.5 us -> 22.8 us
    unnamed x39 -> x18, local copies, waits for them, and re-layouts: 20.4 us -> 3.07 us
    all_to_all x1 -> x0, blocking collectives: 14.2 us -> none  [exchanged(): lax.all_to_all(block, 'bead', split_axis=0, concat_axis=0, tiled=True)]
    all_to_all x2 -> x3, waiting for transfers between devices: 0.63 us -> 11 us  [exchanged(): lax.all_to_all(block, 'bead', split_axis=0, concat_axis=0, tiled=True)]
    pallas_call x1, Pallas kernels: 28 us -> 19.2 us  [on_device(): call(functools.partial(bead_kernel, groups=groups, span=span, block=block...]
    ppermute x4, waiting for transfers between devices: 4.29 us -> 0.01 us  [shifted(): return lax.ppermute(block, ('bead', 'space'), route)]
    all_to_all x2 -> x3, starting transfers between devices: 12 us -> 15.4 us  [exchanged(): lax.all_to_all(block, 'bead', split_axis=0, concat_axis=0, tiled=True)]
    pallas_call x4 -> x6, Pallas kernels: 45.2 us -> 42.6 us  [the longest x1 15.9 us: on_device(): call(functools.partial(inner_kernel, span=span, tiles=inside), f32(2, spa...]
  transfers between devices with their start and end apart: 8 -> 9, of which waited for: 4 -> 4; matrix products, arithmetic and copies ran while one was open for 8% -> 3% of each run, Pallas kernels for 25% -> 42%
where the time goes in v2:
time: 109 us; the launch traced here: 108 us
  Pallas kernels  66.9 us (61%)
  starting transfers between devices  22.8 us (21%)
  waiting for transfers between devices  11.8 us (11%)
  local copies, waits for them, and re-layouts  5.9 us (5%)
    pallas_call x1, Pallas kernels, on_device(): call(functools.partial(bead_kernel, groups=groups, span=span, block=block...  19.2 us
    pallas_call x1, Pallas kernels, on_device(): call(functools.partial(inner_kernel, span=span, tiles=inside), f32(2, spa...  15.9 us
    all_to_all x3, starting transfers between devices, exchanged(): lax.all_to_all(block, 'bead', split_axis=0, concat_axis=0, tiled=True)  15.4 us
    pallas_call x1, Pallas kernels, on_device(): call(functools.partial(outer_kernel, groups=groups, span=span, tiles=outs...  14.4 us
    all_to_all x3, waiting for transfers between devices, exchanged(): lax.all_to_all(block, 'bead', split_axis=0, concat_axis=0, tiled=True)  11 us
    ppermute x4, starting transfers between devices, shifted(): return lax.ppermute(block, ('bead', 'space'), route)  6.85 us
    pallas_call x1, Pallas kernels, on_device(): call(noise_kernel, [f32(size, beads, width)] * 2, [VMEM_SPEC] * 4, scratc...  4.37 us
    unnamed x18, local copies, waits for them, and re-layouts  3.07 us
  transfers between devices with their start and end apart: 9, of which 4 were waited for; matrix products, arithmetic and copies ran while one was open for 3% of the time, Pallas kernels for 42%

profile of v2, /device:TPU:0, one launch (start us, length us, event | category | flops | bytes accessed | tf_op | source)
XLA Modules:
  0.0 108.2 jit_solution(226061442098836010)
XLA Ops:
  0.6 2.3 %shard_map.129 = f32[768,128]{1,0:T(8,128)} custom-call(f32[3,2,8192]{2,1,0:T(2,128)} %bitcast.31, f32[3,2,8192]{2,1,0:T(2,128)} %bitcast.32, f32[3,2,8192]{2,1,0:T(2,128)} %bitcast.33), custom_call_target="tpu_custom_call" | custom-call | tf_op jit(solution)/shard_map/pallas_call | solution.py:500
  2.9 8.3 %all-to-all-start = ((f32[16,48,128]{2,1,0:T(8,128)}), f32[16,48,128]{2,1,0:T(8,128)S(1)}, u32[]{:S(2)}, u32[]{:S(2)}) async-start(f32[16,48,128]{2,1,0:T(8,128)} %bitcast.22), calls=%async_computation | async-start | bytes 786432 | tf_op jit(solution)/shard_map/all_to_all | solution.py:498
  11.2 0.7 reshape.24
  12.0 0.7 copy.16.drift_ref
  12.7 0.7 reshape.25
  13.4 0.7 copy.17.mix_ref
  14.1 4.4 %shard_map.130 = (f32[5,32,1536]{2,1,0:T(8,128)}, f32[5,32,1536]{2,1,0:T(8,128)}) custom-call(f32[32,25]{1,0:T(8,128)} %copy.16.drift_ref, f32[32,25]{1,0:T(8,128)} %copy.17.mix_ref, f32[32,3,4,512]{3,2,1,0:T(4,128)} %bitcast.26, f32[2,5,3,32,512]{4,3,2,1,0:T(8,128)} %bitcast.20), custom_call_target="tpu_custom_call" | custom-call | tf_op jit(solution)/shard_map/pallas_call | solution.py:507
  18.4 5.4 %all-to-all-done = f32[16,48,128]{2,1,0:T(8,128)S(1)} async-done(((f32[16,48,128]{2,1,0:T(8,128)}), f32[16,48,128]{2,1,0:T(8,128)S(1)}, u32[]{:S(2)}, u32[]{:S(2)}) %all-to-all-start) | async-done | bytes 393248 | tf_op jit(solution)/shard_map/all_to_all | solution.py:498
  23.9 0.7 copy-done
  24.6 2.8 %shard_map.131 = (f32[2,2,256,128]{3,2,1,0:T(8,128)}, f32[96,128]{1,0:T(8,128)}, f32[96,128]{1,0:T(8,128)}, f32[96,128]{1,0:T(8,128)}, f32[96,128]{1,0:T(8,128)}...) custom-call(s32[1]{0:T(128)} %bitcast.flag_ref, f32[768,128]{1,0:T(8,128)} %bitcast.21, ...), custom_call_target="tpu_custom_call" | custom-call | tf_op jit(solution)/shard_map/pallas_call | solution.py:516
  27.5 0.6 collective-permute-start
  28.1 1.7 %collective-permute-start.1 = (f32[96,128]{1,0:T(8,128)}, f32[96,128]{1,0:T(8,128)S(1)}, u32[]{:S(2)}, u32[]{:S(2)}) collective-permute-start(f32[96,128]{1,0:T(8,128)} %get-tuple-element.24), channel_id=1, source_target_pairs={{0,2},{1,3},{2,4},{3,5},{4,6},{5,7},{6,8},{7,9},{8,10},{9,11},{10,... | collective-permute-start | bytes 147464 | tf_op jit(solution)/shard_map/ppermute | solution.py:530
  29.8 3.9 %collective-permute-start.2 = (f32[96,128]{1,0:T(8,128)}, f32[96,128]{1,0:T(8,128)S(1)}, u32[]{:S(2)}, u32[]{:S(2)}) collective-permute-start(f32[96,128]{1,0:T(8,128)} %get-tuple-element.25), channel_id=1, source_target_pairs={{0,30},{1,31},{2,0},{3,1},{4,2},{5,3},{6,4},{7,5},{8,6},{9,7},{10,... | collective-permute-start | bytes 147464 | tf_op jit(solution)/shard_map/ppermute | solution.py:530
  33.7 0.6 collective-permute-start.3
  34.3 15.9 %shard_map.132.part_ref = f32[2,2,256,128]{3,2,1,0:T(8,128)} custom-call(f32[2,2,256,128]{3,2,1,0:T(8,128)} %get-tuple-element.22.own_ref), custom_call_target="tpu_custom_call" | custom-call | tf_op jit(solution)/shard_map/pallas_call | solution.py:544
  50.2 3.0 %shard_map.133.base_ref = f32[5,32,1536]{2,1,0:T(8,128)} custom-call(f32[32,1536]{1,0:T(8,128)} %get-tuple-element.29.pm_ref, f32[5,32,1536]{2,1,0:T(8,128)} %get-tuple-element.21.pre_ref.first_ref, f32[5,32,1536]{2,1,0:T(8,128)} %get-tuple-element.30.second_ref, f32[32,25]{1,0:T(8,128)} %copy.16.drift_ref), custom_call_target="tpu_custom_call" | custom-call | tf_op jit(solution)/shard_map/pallas_call | solution.py:550
  53.3 0.6 copy-done.3
  53.9 0.0 copy-done.6
  53.9 14.4 %shard_map.134 = (f32[384,128]{1,0:T(8,128)}, f32[32,1536]{1,0:T(8,128)}, f32[32,1536]{1,0:T(8,128)}) custom-call(f32[2,2,256,128]{3,2,1,0:T(8,128)} %get-tuple-element.22.own_ref, f32[2,2,256,128]{3,2,1,0:T(8,128)} %shard_map.132.part_ref, f32[96,128]{1,0:T(8,128)} %copy-done.3, f32[96,128]{1,0:T(8,128)} %copy-done.4, f32[96,128]{1,0:T(8,128)} %copy-done.5, ...), custom_call_target="tpu_custom_call" | custom-call | tf_op jit(solution)/shard_map/pallas_call | solution.py:551
  68.3 3.5 %all-to-all-start.1 = ((f32[16,24,128]{2,1,0:T(8,128)}), f32[16,24,128]{2,1,0:T(8,128)S(1)}, u32[]{:S(2)}, u32[]{:S(2)}) async-start(f32[16,24,128]{2,1,0:T(8,128)} %bitcast.28), calls=%async_computation.1 | async-start | bytes 393216 | tf_op jit(solution)/shard_map/all_to_all | solution.py:498
  71.8 3.0 %shard_map.136 = (f32[384,128]{1,0:T(8,128)}, f32[32,3,4,512]{3,2,1,0:T(4,128)}) custom-call(f32[32,1536]{1,0:T(8,128)} %get-tuple-element.33.pm_ref, f32[32,1536]{1,0:T(8,128)} %get-tuple-element.34.p0_ref, f32[32,1536]{1,0:T(8,128)} %get-tuple-element.27.qn_ref, f32[5,32,1536]{2,1,0:T(8,128)} %shard_map.133.base_ref, f32[32,32]{1,0:T(8,128)} %constant.13.clone.basis_ref, ...), custom_call_target="tpu_custom_call" | custom-call | tf_op jit(solution)/shard_map/pallas_call | solution.py:562
  74.8 5.6 %all-to-all-done.1 = f32[16,24,128]{2,1,0:T(8,128)S(1)} async-done(((f32[16,24,128]{2,1,0:T(8,128)}), f32[16,24,128]{2,1,0:T(8,128)S(1)}, u32[]{:S(2)}, u32[]{:S(2)}) %all-to-all-start.1) | async-done | bytes 196640 | tf_op jit(solution)/shard_map/all_to_all | solution.py:498
  80.4 3.5 %all-to-all-start.2 = ((f32[16,24,128]{2,1,0:T(8,128)}), f32[16,24,128]{2,1,0:T(8,128)S(1)}, u32[]{:S(2)}, u32[]{:S(2)}) async-start(f32[16,24,128]{2,1,0:T(8,128)} %bitcast.27), calls=%async_computation.2 | async-start | bytes 393216 | tf_op jit(solution)/shard_map/all_to_all | solution.py:498
  83.9 0.1 collective-permute-start.5
  84.0 0.5 collective-permute-start.4
  84.5 0.7 collective-permute-done.5.after_ref
  85.1 0.2 collective-permute-done.4.before_ref
  85.3 0.4 copy-done.7
  85.7 0.6 copy-done.8
  86.3 19.2 %shard_map.135 = (f32[3,2,8192]{2,1,0:T(2,128)}, f32[3,2,8192]{2,1,0:T(2,128)}) custom-call(f32[384,128]{1,0:T(8,128)} %bitcast.24, f32[6,128]{1,0:T(8,128)} %copy-done.8, f32[6,128]{1,0:T(8,128)} %copy-done.7), custom_call_target="tpu_custom_call" | custom-call | tf_op jit(solution)/shard_map/pallas_call | solution.py:576
  105.6 0.7 copy-done.2
  106.3 1.9 %shard_map.137 = f32[3,2,8192]{2,1,0:T(2,128)} custom-call(f32[384,128]{1,0:T(8,128)} %bitcast.25, f32[3,2,8192]{2,1,0:T(2,128)} %get-tuple-element.36.f_ref), custom_call_target="tpu_custom_call" | custom-call | tf_op jit(solution)/shard_map/pallas_call | solution.py:586
  (18 shorter events, 0.1 us)
Async XLA Ops:
  2.9 21.0 %all-to-all-start = ((f32[16,48,128]{2,1,0:T(8,128)}), f32[16,48,128]{2,1,0:T(8,128)S(1)}, u32[]{:S(2)}, u32[]{:S(2)}) async-start(f32[16,48,128]{2,1,0:T(8,128)} %bitcast.22), calls=%async_computation | async-start | bytes 786432 | tf_op jit(solution)/shard_map/all_to_all | solution.py:498
  23.9 0.7 copy-start
  27.5 25.8 %collective-permute-start = (f32[96,128]{1,0:T(8,128)}, f32[96,128]{1,0:T(8,128)S(1)}, u32[]{:S(2)}, u32[]{:S(2)}) collective-permute-start(f32[96,128]{1,0:T(8,128)} %get-tuple-element.23), channel_id=1, source_target_pairs={{0,2},{1,3},{2,4},{3,5},{4,6},{5,7},{6,8},{7,9},{8,10},{9,11},{10,... | collective-permute-start | bytes 147464 | tf_op jit(solution)/shard_map/ppermute | solution.py:530
  28.1 25.2 %collective-permute-start.1 = (f32[96,128]{1,0:T(8,128)}, f32[96,128]{1,0:T(8,128)S(1)}, u32[]{:S(2)}, u32[]{:S(2)}) collective-permute-start(f32[96,128]{1,0:T(8,128)} %get-tuple-element.24), channel_id=1, source_target_pairs={{0,2},{1,3},{2,4},{3,5},{4,6},{5,7},{6,8},{7,9},{8,10},{9,11},{10,... | collective-permute-start | bytes 147464 | tf_op jit(solution)/shard_map/ppermute | solution.py:530
  29.8 23.4 %collective-permute-start.2 = (f32[96,128]{1,0:T(8,128)}, f32[96,128]{1,0:T(8,128)S(1)}, u32[]{:S(2)}, u32[]{:S(2)}) collective-permute-start(f32[96,128]{1,0:T(8,128)} %get-tuple-element.25), channel_id=1, source_target_pairs={{0,30},{1,31},{2,0},{3,1},{4,2},{5,3},{6,4},{7,5},{8,6},{9,7},{10,... | collective-permute-start | bytes 147464 | tf_op jit(solution)/shard_map/ppermute | solution.py:530
  33.7 19.6 %collective-permute-start.3 = (f32[96,128]{1,0:T(8,128)}, f32[96,128]{1,0:T(8,128)S(1)}, u32[]{:S(2)}, u32[]{:S(2)}) collective-permute-start(f32[96,128]{1,0:T(8,128)} %get-tuple-element.26), channel_id=1, source_target_pairs={{0,31},{1,30},{2,0},{3,1},{4,2},{5,3},{6,4},{7,5},{8,6},{9,7},{10,... | collective-permute-start | bytes 147464 | tf_op jit(solution)/shard_map/ppermute | solution.py:530
  53.2 0.6 copy-start.3
  53.2 0.6 copy-start.4
  53.3 0.6 copy-start.5
  53.3 0.6 copy-start.6
  68.3 12.1 %all-to-all-start.1 = ((f32[16,24,128]{2,1,0:T(8,128)}), f32[16,24,128]{2,1,0:T(8,128)S(1)}, u32[]{:S(2)}, u32[]{:S(2)}) async-start(f32[16,24,128]{2,1,0:T(8,128)} %bitcast.28), calls=%async_computation.1 | async-start | bytes 393216 | tf_op jit(solution)/shard_map/all_to_all | solution.py:498
  80.4 4.9 %copy-start.1 = (f32[16,24,128]{2,1,0:T(8,128)}, f32[16,24,128]{2,1,0:T(8,128)S(1)}, u32[]{:S(2)}) copy-start(f32[16,24,128]{2,1,0:T(8,128)S(1)} %all-to-all-done.1) | copy-start | bytes 589828
  80.4 25.2 %all-to-all-start.2 = ((f32[16,24,128]{2,1,0:T(8,128)}), f32[16,24,128]{2,1,0:T(8,128)S(1)}, u32[]{:S(2)}, u32[]{:S(2)}) async-start(f32[16,24,128]{2,1,0:T(8,128)} %bitcast.27), calls=%async_computation.2 | async-start | bytes 393216 | tf_op jit(solution)/shard_map/all_to_all | solution.py:498
  83.9 1.2 %collective-permute-start.5 = (f32[6,128]{1,0:T(8,128)S(1)}, f32[6,128]{1,0:T(8,128)S(1)}, u32[]{:S(2)}, u32[]{:S(2)}) collective-permute-start(f32[6,128]{1,0:T(8,128)S(1)} %get-tuple-element.38), channel_id=1, source_target_pairs={{0,1},{1,0},{2,3},{3,2},{4,5},{5,4},{6,7},{7,6},{8,9},{9,8},{10,11... | collective-permute-start | bytes 9224 | tf_op jit(solution)/shard_map/ppermute | solution.py:573
  84.0 1.3 %collective-permute-start.4 = (f32[6,128]{1,0:T(8,128)S(1)}, f32[6,128]{1,0:T(8,128)S(1)}, u32[]{:S(2)}, u32[]{:S(2)}) collective-permute-start(f32[6,128]{1,0:T(8,128)S(1)} %get-tuple-element.39), channel_id=1, source_target_pairs={{0,1},{1,0},{2,3},{3,2},{4,5},{5,4},{6,7},{7,6},{8,9},{9,8},{10,11... | collective-permute-start | bytes 9224 | tf_op jit(solution)/shard_map/ppermute | solution.py:572
  85.1 0.6 copy-start.7
  85.7 0.6 copy-start.8
  105.6 0.7 copy-start.2

commit v3 on v2

--- a/solution.py
+++ b/solution.py
@@ -78,26 +78,30 @@
 
 def prepare(coords, left_ref, right_ref, slot, want_left, shifts):
     row = lax.broadcasted_iota(jnp.int32, coords.shape, 0)
-
-    def half_square(x):
-        return (0.5 * LOG2E / pair_range) * jnp.sum(x * x, axis=0, keepdims=True)
-
+    scale = LOG2E / pair_range
+    square = (0.5 * scale) * jnp.sum(coords * coords, axis=0, keepdims=True)
+    along = coords[0:1]
     if want_left:
-        x = jnp.where(row == 3, -half_square(coords), coords * (LOG2E / pair_range))
-        x = jnp.where(row == 4, 1.0, x)
+        x = jnp.where(row > 3, 1.0, coords * scale)
+        x = jnp.where(row == 3, -square, x)
+        x = jnp.where(row == 7, along * scale, x)
         a1, a2, a3 = split3(x)
         left = jnp.concatenate([a1, a1, a2, a2, a1, a3], axis=0)
         left_ref[slot] = jnp.transpose(left).astype(jnp.bfloat16)
+    shift = (row - 5).astype(jnp.float32) * cell_length
+    x = jnp.where(row > 3, -square - scale * (shift * along + 0.5 * shift * shift), coords)
+    x = jnp.where(row == 3, 1.0, x)
+    b1, b2, b3 = split3(x)
     for delta in shifts:
-        x = jnp.where(row == 0, coords + delta * cell_length, coords) if delta else coords
-        x = jnp.where(row == 4, -half_square(x), x)
-        x = jnp.where(row == 3, 1.0, x)
-        b1, b2, b3 = split3(x)
-        right_ref[slot, delta + 1] = jnp.concatenate([b1, b2, b1, b2, b3, b1], axis=0).astype(jnp.bfloat16)
-
-
-def pair_scratch(slots, tiles):
-    count = sum(len(of) for of in tiles)
+        keep = (row <= 3) | (row == 5 + delta)
+        c1 = jnp.where(keep, b1, jnp.where(row == 7, delta * cell_length, 0.0))
+        c2 = jnp.where(keep, b2, 0.0)
+        c3 = jnp.where(keep, b3, 0.0)
+        right_ref[slot, delta + 1] = jnp.concatenate([c1, c2, c1, c2, c3, c1], axis=0).astype(jnp.bfloat16)
+
+
+def pair_scratch(slots, units):
+    count = sum(len(others) for _, _, others in units)
     return [
         pltpu.VMEM((slots, CELL_ATOMS, 48), jnp.bfloat16),
         pltpu.VMEM((slots, 3, 48, CELL_ATOMS), jnp.bfloat16),
@@ -108,48 +112,46 @@
     ]
 
 
-def pair_sums(steps, tiles, base_of, finish, left_ref, right_ref, e0_ref, e1_ref, w0_ref, w1_ref):
+def pair_sums(steps, units, base_of, finish, left_ref, right_ref, e0_ref, e1_ref, w0_ref, w1_ref):
     n = CELL_ATOMS
 
     def powers(step, e_ref):
         base = base_of(step)
         at = 0
-        for u, of in enumerate(tiles):
-            for offset, delta in of:
+        for _, center, others in units:
+            for offset, delta in others:
                 e_ref[at * n : (at + 1) * n] = jnp.dot(
                     left_ref[base + offset],
-                    right_ref[base + 1 + u, 1 - delta],
+                    right_ref[base + center, 1 - delta],
                     preferred_element_type=jnp.float32,
                 )
                 at += 1
 
     def weights(e_ref, w_ref):
         at = 0
-        for of in tiles:
-            for number in range(len(of)):
+        for _, _, others in units:
+            for number in range(len(others)):
                 weight = jnp.exp2(e_ref[(at + number) * n : (at + number + 1) * n])
                 high = weight.astype(jnp.bfloat16)
                 low = (weight - high.astype(jnp.float32)).astype(jnp.bfloat16)
                 place = 2 * at + number
                 w_ref[place * n : (place + 1) * n] = high
-                place += len(of)
+                place += len(others)
                 w_ref[place * n : (place + 1) * n] = low
-            at += len(of)
+            at += len(others)
 
     def sums(step, w_ref):
         base = base_of(step)
         at = 0
-        for u, of in enumerate(tiles):
-            if not of:
-                continue
-            rows = [right_ref[base + offset, delta + 1, 0:16] for offset, delta in of]
+        for tag, _, others in units:
+            rows = [right_ref[base + offset, delta + 1, 0:16] for offset, delta in others]
             total = jnp.dot(
                 jnp.concatenate(rows + rows, axis=1),
-                w_ref[2 * at * n : 2 * (at + len(of)) * n],
+                w_ref[2 * at * n : 2 * (at + len(others)) * n],
                 preferred_element_type=jnp.float32,
             )
-            finish(step, u, total[:8] + total[8:])
-            at += len(of)
+            finish(step, tag, total[:8] + total[8:])
+            at += len(others)
 
     def clamp(step):
         return jnp.clip(step, 0, steps - 1)
@@ -167,6 +169,12 @@
     lax.fori_loop(0, (steps + 3) // 2, pair, 0)
 
 
+def coefficient(center, sums):
+    row = lax.broadcasted_iota(jnp.int32, sums.shape, 0)
+    pulled = jnp.where(row == 0, sums + sums[7:8], sums)
+    return (pair_strength / pair_range) * (center * sums[3:4] - pulled)
+
+
 def place_loop(groups, span, one):
     def body(b, carry):
         for h in range(2):
@@ -201,7 +209,7 @@
     return [(t, c, slice((t * 3 + c) * LANES, (t * 3 + c + 1) * LANES)) for t in range(tiles) for c in range(3)]
 
 
-def noise_kernel(drift_ref, mix_ref, aux_ref, noise_ref, first_ref, second_ref, rows_ref):
+def noise_kernel(drift_ref, mix_ref, aux_ref, noise_ref, first_ref, later_ref, rows_ref):
     beads = aux_ref.shape[0]
     size = AUX + 1
     tiles = aux_ref.shape[3] // LANES
@@ -215,20 +223,37 @@
     lax.fori_loop(0, beads, copy, 0)
     drift = drift_ref[...]
     mix = mix_ref[...]
+
+    def mixed(s, a, c, inner):
+        at = a * size
+        total = mix[:, at : at + 1] * noise_ref[s, 0, c, :, inner]
+        for b in range(1, size):
+            total = total + mix[:, at + b : at + b + 1] * noise_ref[s, b, c, :, inner]
+        return total
+
     for t, c, lanes in columns_of(tiles):
         inner = slice(t * LANES, (t + 1) * LANES)
         others = [rows_ref[c, t, pl.ds(b, beads, stride=AUX), :] for b in range(AUX)]
-        for s, ref in ((0, first_ref), (1, second_ref)):
-            noises = [noise_ref[s, b, c, :, inner] for b in range(size)]
-            for a in range(size):
-                at = a * size
-                total = mix[:, at : at + 1] * noises[0]
-                for b in range(1, size):
-                    total = total + mix[:, at + b : at + b + 1] * noises[b]
-                if s == 0:
-                    for b in range(AUX):
-                        total = total + drift[:, at + b + 1 : at + b + 2] * others[b]
-                ref[a, :, lanes] = total
+        news = []
+        for a in range(size):
+            total = mixed(0, a, c, inner)
+            for b in range(AUX):
+                total = total + drift[:, a * size + b + 1 : a * size + b + 2] * others[b]
+            news.append(total)
+        first_ref[:, lanes] = news[0]
+        for a in range(size):
+            total = mixed(1, a, c, inner)
+            for b in range(1, size):
+                total = total + drift[:, a * size + b : a * size + b + 1] * news[b]
+            later_ref[a, :, lanes] = total
+
+
+def twice(drift, a):
+    size = AUX + 1
+    total = drift[:, a * size + 1 : a * size + 2] * drift[:, size : size + 1]
+    for b in range(2, size):
+        total = total + drift[:, a * size + b : a * size + b + 1] * drift[:, b * size : b * size + 1]
+    return total
 
 
 def strided(ref, start, size, stride):
@@ -265,7 +290,7 @@
     gather = gather_ref[...]
     qm = dot(gather, gathered(0))
     pm = dot(gather, gathered(1))
-    p0 = drift_ref[:, 0:1] * pm + pre_ref[0]
+    p0 = drift_ref[:, 0:1] * pm + pre_ref[...]
     qn, pn = turned(qm, p0, turn_ref[...])
     new = dot(basis_ref[...], qn)
     own_ref[...] = jnp.zeros_like(own_ref)
@@ -287,25 +312,7 @@
     pm_ref[...] = pm
 
 
-def middle_kernel(pm_ref, first_ref, second_ref, drift_ref, out_ref):
-    size = AUX + 1
-    drift = drift_ref[...]
-    for at in range(0, pm_ref.shape[1], LANES):
-        lanes = slice(at, at + LANES)
-        pm = pm_ref[:, lanes]
-        aux = [drift[:, a * size : a * size + 1] * pm + first_ref[a, :, lanes] for a in range(1, size)]
-        for a in range(size):
-            total = second_ref[a, :, lanes]
-            for b in range(AUX):
-                total = total + drift[:, a * size + b + 1 : a * size + b + 2] * aux[b]
-            out_ref[a, :, lanes] = total
-
-
-def coefficient(center, sums):
-    return (pair_strength / pair_range) * (center * sums[3:4] - sums)
-
-
-def inner_kernel(own_ref, force_ref, *scratch, span, tiles):
+def inner_kernel(own_ref, force_ref, *scratch, span, runs, units):
     beads = own_ref.shape[2] // 8
     left_ref, right_ref = scratch[:2]
 
@@ -323,17 +330,18 @@
 
     lax.fori_loop(0, beads, one, 0)
 
-    def finish(step, u, sums):
-        h, here = step % 2, tile(step // 2)
+    def finish(step, tag, sums):
+        run, u = tag
+        h, here = run % 2, tile(step * (runs // 2) + run // 2)
         force_ref[h, u, here, :] = coefficient(own_ref[h, u, here, :], sums)
 
-    pair_sums(2 * beads, tiles, lambda step: step * (span + 2), finish, *scratch)
+    pair_sums(2 * beads // runs, units, lambda step: step * (runs * (span + 2)), finish, *scratch)
 
 
 def outer_kernel(
-    own_ref, part_ref, up0_ref, up1_ref, dn0_ref, dn1_ref, qn_ref, pn_ref, base_ref,
+    own_ref, part_ref, up0_ref, up1_ref, dn0_ref, dn1_ref, qn_ref, pn_ref, pm1_ref, later_ref,
     gather_ref, basis_ref, turn_ref, drift_ref,
-    sendq_ref, pm_ref, p0_ref, halo_ref, force_ref, *scratch, groups, span, tiles,
+    send_ref, pm_ref, halo_ref, force_ref, *scratch, groups, span, runs, units,
 ):
     beads = basis_ref.shape[0]
     here = beads // groups
@@ -353,57 +361,49 @@
             prepare(halo_ref[h, at, :], left_ref, right_ref, slot, True, (-1,))
             prepare(halo_ref[2 + h, at, :], left_ref, right_ref, slot + span + 1, True, (1,))
             for u in sorted({0, span - 1}):
-                shifts = tuple(sorted(-delta for _, delta in tiles[u]))
+                shifts = ((1,) if u == 0 else ()) + ((-1,) if u == span - 1 else ())
                 prepare(own_ref[h, u, at, :], left_ref, right_ref, slot + u + 1, False, shifts)
         return carry
 
     lax.fori_loop(0, beads, one, 0)
     force_ref[...] = part_ref[...]
 
-    def finish(step, u, sums):
-        h, at = step % 2, tile(step // 2)
+    def finish(step, tag, sums):
+        run, u = tag
+        h, at = run % 2, tile(step * (runs // 2) + run // 2)
         force_ref[h, u, at, :] = part_ref[h, u, at, :] + coefficient(own_ref[h, u, at, :], sums)
 
-    pair_sums(2 * beads, tiles, lambda step: step * (span + 2), finish, *scratch)
+    pair_sums(2 * beads // runs, units, lambda step: step * (runs * (span + 2)), finish, *scratch)
 
     force = jnp.concatenate(
         [strided(force_ref.at[t // span, t % span], c, beads, 8) for t, c, _ in columns_of(2 * span)], axis=1
     )
     pm = pn_ref[...] + time_step * dot(gather_ref[...], force)
-    p0 = drift_ref[:, 0:1] * pm + base_ref[0]
-    qn, _ = turned(qn_ref[...], p0, turn_ref[...])
-    new = dot(basis_ref[...], qn)
+    drift = drift_ref[...]
+    p0 = drift[:, 0:1] * pm + (twice(drift, 0) * pm1_ref[...] + later_ref[...])
+    qn, pn = turned(qn_ref[...], p0, turn_ref[...])
     count = 6 * span
-    for number in range(count):
-        for j in range(here):
-            sendq_ref[pl.ds(number * here + j, groups, stride=count * here), :] = new[
-                j * groups : (j + 1) * groups, number * LANES : (number + 1) * LANES
-            ]
+    for which, modes in enumerate((qn, pn)):
+        new = dot(basis_ref[...], modes)
+        for number in range(count):
+            for j in range(here):
+                place = pl.ds((which * count + number) * here + j, groups, stride=2 * count * here)
+                send_ref[place, :] = new[j * groups : (j + 1) * groups, number * LANES : (number + 1) * LANES]
     pm_ref[...] = pm
-    p0_ref[...] = p0
-
-
-def rest_kernel(
-    pm_ref, p0_ref, qn_ref, base_ref, basis_ref, turn_ref, drift_ref,
-    sendp_ref, out_ref, rows_ref, *, groups, span,
-):
-    beads = basis_ref.shape[0]
-    here = beads // groups
+
+
+def rest_kernel(pm1_ref, pm_ref, later_ref, drift_ref, out_ref, rows_ref, *, span):
+    beads = pm_ref.shape[0]
     size = AUX + 1
-    _, pn = turned(qn_ref[...], p0_ref[...], turn_ref[...])
-    new = dot(basis_ref[...], pn)
-    count = 6 * span
-    for number in range(count):
-        for j in range(here):
-            sendp_ref[pl.ds(number * here + j, groups, stride=count * here), :] = new[
-                j * groups : (j + 1) * groups, number * LANES : (number + 1) * LANES
-            ]
     drift = drift_ref[...]
+    again = [twice(drift, a) for a in range(1, size)]
     for t, c, lanes in columns_of(2 * span):
+        pm1 = pm1_ref[:, lanes]
         pm = pm_ref[:, lanes]
-        for a in range(AUX):
-            at = (a + 1) * size
-            rows_ref[c, t, pl.ds(a, beads, stride=AUX), :] = drift[:, at : at + 1] * pm + base_ref[a + 1, :, lanes]
+        for a in range(1, size):
+            rows_ref[c, t, pl.ds(a - 1, beads, stride=AUX), :] = drift[:, a * size : a * size + 1] * pm + (
+                again[a - 1] * pm1 + later_ref[a, :, lanes]
+            )
 
     def copy(k, carry):
         for c in range(3):
@@ -414,8 +414,12 @@
     lax.fori_loop(0, beads, copy, 0)
 
 
-def bead_kernel(got_ref, before_ref, after_ref, q_ref, f_ref, x_ref, force_ref, *scratch, groups, span, block, tiles):
+def bead_kernel(
+    got_ref, before_ref, after_ref, q_ref, p_ref, f_ref, x_ref, force_ref, *scratch, groups, span, block, units
+):
     here = q_ref.shape[1]
+    half = 0.5 * time_step
+    rows = 6 * span * here
     cells = q_ref.shape[2] // LANES
     left_ref, right_ref = scratch[:2]
     x_ref[...] = jnp.zeros_like(x_ref)
@@ -424,7 +428,7 @@
         x_ref[(j + 1) * (cells + 2) - 1, 0:3] = strided(after_ref, j, 3, here)
 
     def place(b, tile, cell):
-        row = (b * 2 * span + tile) * 3 * here
+        row = b * 2 * rows + tile * 3 * here
         for c in range(3):
             q_ref[c, :, lanes_of(cell)] = got_ref[pl.ds(row + c * here, here), :]
         for j in range(here):
@@ -450,27 +454,16 @@
         at = pl.multiple_of((step * block + u) * 8, 8)
         force_ref[pl.ds(at, 8), :] = coefficient(x_ref[base_of(step) + 1 + u], sums)
 
-    pair_sums(here * per_bead, tiles, base_of, finish, *scratch)
-
-    def out(cell, carry):
+    pair_sums(here * per_bead, units, base_of, finish, *scratch)
+
+    def out(b, tile, cell):
+        row = b * 2 * rows + rows + tile * 3 * here
         for c in range(3):
-            f_ref[c, :, lanes_of(cell)] = strided(force_ref, cell * 8 + c, here, cells * 8)
-        return carry
-
-    lax.fori_loop(0, cells, out, 0)
-
-
-def last_kernel(got_ref, f_ref, out_ref, *, groups, span):
-    here = f_ref.shape[1]
-    half = 0.5 * time_step
-
-    def one(b, tile, cell):
-        lanes = lanes_of(cell)
-        row = (b * 2 * span + tile) * 3 * here
-        for c in range(3):
-            out_ref[c, :, lanes] = got_ref[pl.ds(row + c * here, here), :] + half * f_ref[c, :, lanes]
-
-    place_loop(groups, span, one)
+            force = strided(force_ref, cell * 8 + c, here, cells * 8)
+            f_ref[c, :, lanes_of(cell)] = force
+            p_ref[c, :, lanes_of(cell)] = got_ref[pl.ds(row + c * here, here), :] + half * force
+
+    place_loop(groups, span, out)
 
 
 def on_device(positions, momenta, forces, gle_drift, gle_noise_mix, aux_momenta, noise):
@@ -504,9 +497,9 @@
     )(by_coord(positions), by_coord(momenta), by_coord(forces))
     got = exchanged(send)
     rows = pltpu.VMEM((3, 2 * span, beads * AUX, LANES), jnp.float32)
-    first, second = call(
+    first, later = call(
         noise_kernel,
-        [f32(size, beads, width)] * 2,
+        [f32(beads, width), f32(size, beads, width)],
         [VMEM_SPEC] * 4,
         scratch_shapes=[rows],
     )(drift, mix, jnp.transpose(aux_momenta, (0, 2, 1, 3)), jnp.transpose(noise, (0, 2, 3, 1, 4)))
@@ -535,59 +528,56 @@
     dn1 = shifted(dn1, -1, -1)
 
     slots = 2 * beads * (span + 2)
-    inside = [
-        [(v + 1, v - u) for v in range(span) if abs(v - u) <= 1] for u in range(span)
-    ]
-    outside = [
-        ([(0, -1)] if u == 0 else []) + ([(span + 1, 1)] if u == span - 1 else []) for u in range(span)
-    ]
+    inside, outside = [], []
+    inside_runs, outside_runs = math.gcd(2 * beads, 4), math.gcd(2 * beads, 8)
+    for runs, units, near in ((inside_runs, inside, range(span)), (outside_runs, outside, (-1, span))):
+        for run in range(runs):
+            for u in range(span):
+                at = run * (span + 2) + 1
+                others = [(at + v, v - u) for v in near if abs(v - u) <= 1]
+                if others:
+                    units.append(((run, u), at + u, others))
     part = call(
-        functools.partial(inner_kernel, span=span, tiles=inside),
+        functools.partial(inner_kernel, span=span, runs=inside_runs, units=inside),
         f32(2, span, beads * 8, LANES),
         [VMEM_SPEC],
         scratch_shapes=pair_scratch(slots, inside),
     )(own)
-    base = call(middle_kernel, f32(size, beads, width), [VMEM_SPEC] * 4)(pm, first, second, drift)
-    sendq, pm, p0 = call(
-        functools.partial(outer_kernel, groups=groups, span=span, tiles=outside),
-        [f32(beads * columns, LANES), state, state],
-        [VMEM_SPEC] * 13,
+    send, pm2 = call(
+        functools.partial(outer_kernel, groups=groups, span=span, runs=outside_runs, units=outside),
+        [f32(2 * beads * columns, LANES), state],
+        [VMEM_SPEC] * 14,
         scratch_shapes=[
             pltpu.VMEM((4, beads * 8, LANES), jnp.float32),
             pltpu.VMEM((2, span, beads * 8, LANES), jnp.float32),
         ]
         + pair_scratch(slots, outside),
-    )(own, part, up0, up1, dn0, dn1, qn, pn, base, gather, basis, turn, drift)
-    gotq = exchanged(sendq)
-    sendp, aux_out = call(
-        functools.partial(rest_kernel, groups=groups, span=span),
-        [f32(beads * columns, LANES), f32(beads, 3, AUX, aux_momenta.shape[3])],
-        [VMEM_SPEC] * 7,
+    )(own, part, up0, up1, dn0, dn1, qn, pn, pm, later[0], gather, basis, turn, drift)
+    got = exchanged(send)
+    aux_out = call(
+        functools.partial(rest_kernel, span=span),
+        f32(beads, 3, AUX, aux_momenta.shape[3]),
+        [VMEM_SPEC] * 4,
         scratch_shapes=[rows],
-    )(pm, p0, qn, base, basis, turn, drift)
-    gotp = exchanged(sendp)
-
-    head = gotq[: 3 * here]
-    tail = gotq[-3 * here :]
+    )(pm, pm2, later, drift)
+
+    head = got[: 3 * here]
+    end = (2 * groups - 1) * here * columns
+    tail = got[end - 3 * here : end]
     before = lax.ppermute(tail, "space", [(s, (s + 1) % spaces) for s in range(spaces)])
     after = lax.ppermute(head, "space", [(s, (s - 1) % spaces) for s in range(spaces)])
-    block = math.gcd(cells, 2)
-    around = [[(u, -1), (u + 1, 0), (u + 2, 1)] for u in range(block)]
-    new_q, new_f = call(
-        functools.partial(bead_kernel, groups=groups, span=span, block=block, tiles=around),
-        [grid] * 2,
+    block = math.gcd(cells, 4)
+    around = [(u, u + 1, [(u, -1), (u + 1, 0), (u + 2, 1)]) for u in range(block)]
+    new_q, new_p, new_f = call(
+        functools.partial(bead_kernel, groups=groups, span=span, block=block, units=around),
+        [grid] * 3,
         [VMEM_SPEC] * 3,
         scratch_shapes=[
             pltpu.VMEM((here * (cells + 2), 8, LANES), jnp.float32),
             pltpu.VMEM((here * cells * 8, LANES), jnp.float32),
         ]
         + pair_scratch(here * (cells + 2), around),
-    )(gotq, before, after)
-    new_p = call(
-        functools.partial(last_kernel, groups=groups, span=span),
-        grid,
-        [VMEM_SPEC] * 2,
-    )(gotp, new_f)
+    )(got, before, after)
     return by_coord(new_q), by_coord(new_p), by_coord(new_f), jnp.transpose(aux_out, (0, 2, 1, 3))
 
 

time: 109 us -> 103 us (0.945)
  blocking collectives: 0 us -> 16.1 us
  Pallas kernels: 66.9 us -> 58 us
  starting transfers between devices: 22.8 us -> 15.7 us
  waiting for transfers between devices: 11.8 us -> 5.16 us
  local copies, waits for them, and re-layouts: 5.9 us -> 7 us
    all_to_all x0 -> x1, blocking collectives: none -> 16.1 us  [exchanged(): lax.all_to_all(block, 'bead', split_axis=0, concat_axis=0, tiled=True)]
    pallas_call x6 -> x4, Pallas kernels: 42.6 us -> 34.9 us  [the longest x1 14.6 us: on_device(): call(functools.partial(inner_kernel, span=span, runs=inside_runs, units=i...]
    all_to_all x3 -> x1, starting transfers between devices: 15.4 us -> 8.34 us  [exchanged(): lax.all_to_all(block, 'bead', split_axis=0, concat_axis=0, tiled=True)]
    all_to_all x3 -> x1, waiting for transfers between devices: 11 us -> 5.14 us  [exchanged(): lax.all_to_all(block, 'bead', split_axis=0, concat_axis=0, tiled=True)]
    squeeze x0 -> x1, local copies, waits for them, and re-layouts: none -> 1.62 us  [on_device(): later[0]]
    pallas_call x1, Pallas kernels: 19.2 us -> 18.1 us  [on_device(): call(functools.partial(bead_kernel, groups=groups, span=span, block=block...]
    unnamed x18 -> x16, local copies, waits for them, and re-layouts: 3.07 us -> 2.55 us
  transfers between devices with their start and end apart: 9 -> 7, of which waited for: 4 -> 1; matrix products, arithmetic and copies ran while one was open for 3% -> 4% of each run, Pallas kernels for 42% -> 22%
where the time goes in v3:
time: 103 us
  Pallas kernels  58 us (56%)
  blocking collectives  16.1 us (16%)
  starting transfers between devices  15.7 us (15%)
  local copies, waits for them, and re-layouts  7 us (7%)
  waiting for transfers between devices  5.16 us (5%)
    pallas_call x1, Pallas kernels, on_device(): call(functools.partial(bead_kernel, groups=groups, span=span, block=block...  18.1 us
    all_to_all x1, blocking collectives, exchanged(): lax.all_to_all(block, 'bead', split_axis=0, concat_axis=0, tiled=True)  16.1 us
    pallas_call x1, Pallas kernels, on_device(): call(functools.partial(inner_kernel, span=span, runs=inside_runs, units=i...  14.6 us
    pallas_call x1, Pallas kernels, on_device(): call(functools.partial(outer_kernel, groups=groups, span=span, runs=outsi...  12.6 us
    all_to_all x1, starting transfers between devices, exchanged(): lax.all_to_all(block, 'bead', split_axis=0, concat_axis=0, tiled=True)  8.34 us
    ppermute x4, starting transfers between devices, shifted(): return lax.ppermute(block, ('bead', 'space'), route)  6.85 us
    all_to_all x1, waiting for transfers between devices, exchanged(): lax.all_to_all(block, 'bead', split_axis=0, concat_axis=0, tiled=True)  5.14 us
    pallas_call x1, Pallas kernels, on_device(): call(noise_kernel, [f32(beads, width), f32(size, beads, width)], [VMEM_SP...  4.64 us
  transfers between devices with their start and end apart: 7, of which 1 were waited for; matrix products, arithmetic and copies ran while one was open for 4% of the time, Pallas kernels for 22%

profile of v3, /device:TPU:0, one launch (start us, length us, event | category | flops | bytes accessed | tf_op | source)
XLA Modules:
  0.0 102.6 jit_solution(14516856909408799911)
XLA Ops:
  0.6 2.3 %shard_map.129 = f32[768,128]{1,0:T(8,128)} custom-call(f32[3,2,8192]{2,1,0:T(2,128)} %bitcast.28, f32[3,2,8192]{2,1,0:T(2,128)} %bitcast.29, f32[3,2,8192]{2,1,0:T(2,128)} %bitcast.30), custom_call_target="tpu_custom_call" | custom-call | tf_op jit(solution)/shard_map/pallas_call | solution.py:493
  2.9 8.3 %all-to-all-start = ((f32[16,48,128]{2,1,0:T(8,128)}), f32[16,48,128]{2,1,0:T(8,128)S(1)}, u32[]{:S(2)}, u32[]{:S(2)}) async-start(f32[16,48,128]{2,1,0:T(8,128)} %bitcast.24), calls=%async_computation | async-start | bytes 786432 | tf_op jit(solution)/shard_map/all_to_all | solution.py:491
  11.2 0.7 reshape.22
  12.0 0.7 copy.16.drift_ref
  12.7 0.7 reshape.23
  13.4 0.7 copy.17.mix_ref
  14.1 4.6 %shard_map.130 = (f32[32,1536]{1,0:T(8,128)}, f32[5,32,1536]{2,1,0:T(8,128)}) custom-call(f32[32,25]{1,0:T(8,128)} %copy.16.drift_ref, f32[32,25]{1,0:T(8,128)} %copy.17.mix_ref, f32[32,3,4,512]{3,2,1,0:T(4,128)} %bitcast.26, f32[2,5,3,32,512]{4,3,2,1,0:T(8,128)} %bitcast.20), custom_call_target="tpu_custom_call" | custom-call | tf_op jit(solution)/shard_map/pallas_call | solution.py:500
  18.7 5.1 %all-to-all-done = f32[16,48,128]{2,1,0:T(8,128)S(1)} async-done(((f32[16,48,128]{2,1,0:T(8,128)}), f32[16,48,128]{2,1,0:T(8,128)S(1)}, u32[]{:S(2)}, u32[]{:S(2)}) %all-to-all-start) | async-done | bytes 393248 | tf_op jit(solution)/shard_map/all_to_all | solution.py:491
  23.9 0.8 copy-done.1
  24.6 2.7 %shard_map.131 = (f32[2,2,256,128]{3,2,1,0:T(8,128)}, f32[96,128]{1,0:T(8,128)}, f32[96,128]{1,0:T(8,128)}, f32[96,128]{1,0:T(8,128)}, f32[96,128]{1,0:T(8,128)}...) custom-call(s32[1]{0:T(128)} %bitcast.flag_ref, f32[768,128]{1,0:T(8,128)} %bitcast.23, ...), custom_call_target="tpu_custom_call" | custom-call | tf_op jit(solution)/shard_map/pallas_call | solution.py:509
  27.3 0.6 collective-permute-start
  27.9 1.7 %collective-permute-start.1 = (f32[96,128]{1,0:T(8,128)}, f32[96,128]{1,0:T(8,128)S(1)}, u32[]{:S(2)}, u32[]{:S(2)}) collective-permute-start(f32[96,128]{1,0:T(8,128)} %get-tuple-element.22), channel_id=1, source_target_pairs={{0,2},{1,3},{2,4},{3,5},{4,6},{5,7},{6,8},{7,9},{8,10},{9,11},{10,... | collective-permute-start | bytes 147464 | tf_op jit(solution)/shard_map/ppermute | solution.py:523
  29.6 3.9 %collective-permute-start.2 = (f32[96,128]{1,0:T(8,128)}, f32[96,128]{1,0:T(8,128)S(1)}, u32[]{:S(2)}, u32[]{:S(2)}) collective-permute-start(f32[96,128]{1,0:T(8,128)} %get-tuple-element.23), channel_id=1, source_target_pairs={{0,30},{1,31},{2,0},{3,1},{4,2},{5,3},{6,4},{7,5},{8,6},{9,7},{10,... | collective-permute-start | bytes 147464 | tf_op jit(solution)/shard_map/ppermute | solution.py:523
  33.5 0.6 collective-permute-start.3
  34.1 1.6 %slice_bitcast_fusion.later_ref = f32[32,1536]{1,0:T(8,128)} fusion(f32[5,32,1536]{2,1,0:T(8,128)} %get-tuple-element.28.later_ref), kind=kLoop, calls=%fused_computation | loop fusion | bytes 393216 | tf_op jit(solution)/shard_map/squeeze | solution.py:555
  35.7 14.6 %shard_map.132.part_ref = f32[2,2,256,128]{3,2,1,0:T(8,128)} custom-call(f32[2,2,256,128]{3,2,1,0:T(8,128)} %get-tuple-element.20.own_ref), custom_call_target="tpu_custom_call" | custom-call | tf_op jit(solution)/shard_map/pallas_call | solution.py:540
  50.4 0.0 collective-permute-done.up0_ref
  50.4 0.0 collective-permute-done.1.up1_ref
  50.4 0.0 collective-permute-done.3.dn1_ref
  50.4 0.6 copy-done.2
  51.0 0.0 copy-done.3
  51.0 0.0 copy-done.4
  51.0 0.0 copy-done.5
  51.1 12.6 %shard_map.133 = (f32[768,128]{1,0:T(8,128)}, f32[32,1536]{1,0:T(8,128)}) custom-call(f32[2,2,256,128]{3,2,1,0:T(8,128)} %get-tuple-element.20.own_ref, f32[2,2,256,128]{3,2,1,0:T(8,128)} %shard_map.132.part_ref, f32[96,128]{1,0:T(8,128)} %copy-done.2, f32[96,128]{1,0:T(8,128)} %copy-done.3, f32[96,128]{1,0:T(8,128)} %copy-done.4, f32[96,128]{1,0:T(8,128)} %copy-done.5, ...), custom_call_target="tpu_custom_call" | custom-call | tf_op jit(solution)/shard_map/pallas_call | solution.py:546
  63.7 16.1 %all_to_all.22 = f32[16,48,128]{2,1,0:T(8,128)S(1)} all-to-all(f32[16,48,128]{2,1,0:T(8,128)} %bitcast.27), channel_id=1, replica_groups=mesh['bead'=16,'space'=2] {'bead'}, dimensions={0} | all-to-all | bytes 786432 | tf_op jit(solution)/shard_map/all_to_all | solution.py:491
  79.7 0.0 collective-permute-start.5
  79.7 0.5 collective-permute-start.4
  80.2 3.0 %shard_map.135 = f32[32,3,4,512]{3,2,1,0:T(4,128)} custom-call(f32[32,1536]{1,0:T(8,128)} %get-tuple-element.27.pm1_ref, f32[32,1536]{1,0:T(8,128)} %get-tuple-element.33.pm_ref, f32[5,32,1536]{2,1,0:T(8,128)} %get-tuple-element.28.later_ref, f32[32,25]{1,0:T(8,128)} %copy.16.drift_ref), custom_call_target="tpu_custom_call" | custom-call | tf_op jit(solution)/shard_map/pallas_call | solution.py:557
  83.3 0.0 collective-permute-done.4.before_ref
  83.3 0.6 copy-done.6
  83.9 0.6 copy-done.7
  84.5 18.1 %shard_map.134 = (f32[3,2,8192]{2,1,0:T(2,128)}, f32[3,2,8192]{2,1,0:T(2,128)}, f32[3,2,8192]{2,1,0:T(2,128)}) custom-call(f32[768,128]{1,0:T(8,128)} %bitcast.22, f32[6,128]{1,0:T(8,128)} %copy-done.7, f32[6,128]{1,0:T(8,128)} %copy-done.6), custom_call_target="tpu_custom_call" | custom-call | tf_op jit(solution)/shard_map/pallas_call | solution.py:571
  (12 shorter events, 0.0 us)
Async XLA Ops:
  2.9 21.0 %all-to-all-start = ((f32[16,48,128]{2,1,0:T(8,128)}), f32[16,48,128]{2,1,0:T(8,128)S(1)}, u32[]{:S(2)}, u32[]{:S(2)}) async-start(f32[16,48,128]{2,1,0:T(8,128)} %bitcast.24), calls=%async_computation | async-start | bytes 786432 | tf_op jit(solution)/shard_map/all_to_all | solution.py:491
  23.9 0.8 copy-start.1
  27.3 23.1 %collective-permute-start = (f32[96,128]{1,0:T(8,128)}, f32[96,128]{1,0:T(8,128)S(1)}, u32[]{:S(2)}, u32[]{:S(2)}) collective-permute-start(f32[96,128]{1,0:T(8,128)} %get-tuple-element.21), channel_id=1, source_target_pairs={{0,2},{1,3},{2,4},{3,5},{4,6},{5,7},{6,8},{7,9},{8,10},{9,11},{10,... | collective-permute-start | bytes 147464 | tf_op jit(solution)/shard_map/ppermute | solution.py:523
  27.9 22.5 %collective-permute-start.1 = (f32[96,128]{1,0:T(8,128)}, f32[96,128]{1,0:T(8,128)S(1)}, u32[]{:S(2)}, u32[]{:S(2)}) collective-permute-start(f32[96,128]{1,0:T(8,128)} %get-tuple-element.22), channel_id=1, source_target_pairs={{0,2},{1,3},{2,4},{3,5},{4,6},{5,7},{6,8},{7,9},{8,10},{9,11},{10,... | collective-permute-start | bytes 147464 | tf_op jit(solution)/shard_map/ppermute | solution.py:523
  29.6 20.8 %collective-permute-start.2 = (f32[96,128]{1,0:T(8,128)}, f32[96,128]{1,0:T(8,128)S(1)}, u32[]{:S(2)}, u32[]{:S(2)}) collective-permute-start(f32[96,128]{1,0:T(8,128)} %get-tuple-element.23), channel_id=1, source_target_pairs={{0,30},{1,31},{2,0},{3,1},{4,2},{5,3},{6,4},{7,5},{8,6},{9,7},{10,... | collective-permute-start | bytes 147464 | tf_op jit(solution)/shard_map/ppermute | solution.py:523
  33.5 16.9 %collective-permute-start.3 = (f32[96,128]{1,0:T(8,128)}, f32[96,128]{1,0:T(8,128)S(1)}, u32[]{:S(2)}, u32[]{:S(2)}) collective-permute-start(f32[96,128]{1,0:T(8,128)} %get-tuple-element.24), channel_id=1, source_target_pairs={{0,31},{1,30},{2,0},{3,1},{4,2},{5,3},{6,4},{7,5},{8,6},{9,7},{10,... | collective-permute-start | bytes 147464 | tf_op jit(solution)/shard_map/ppermute | solution.py:523
  50.4 0.6 copy-start.2
  50.4 0.6 copy-start.3
  50.4 0.6 copy-start.4
  50.4 0.6 copy-start.5
  79.7 3.6 %copy-start = (f32[16,48,128]{2,1,0:T(8,128)}, f32[16,48,128]{2,1,0:T(8,128)S(1)}, u32[]{:S(2)}) copy-start(f32[16,48,128]{2,1,0:T(8,128)S(1)} %all_to_all.22) | copy-start | bytes 1179652
  79.7 3.6 %collective-permute-start.5 = (f32[6,128]{1,0:T(8,128)S(1)}, f32[6,128]{1,0:T(8,128)S(1)}, u32[]{:S(2)}, u32[]{:S(2)}) collective-permute-start(f32[6,128]{1,0:T(8,128)S(1)} %get-tuple-element.34), channel_id=1, source_target_pairs={{0,1},{1,0},{2,3},{3,2},{4,5},{5,4},{6,7},{7,6},{8,9},{9,8},{10,11... | collective-permute-start | bytes 9224 | tf_op jit(solution)/shard_map/ppermute | solution.py:568
  79.7 3.6 %collective-permute-start.4 = (f32[6,128]{1,0:T(8,128)S(1)}, f32[6,128]{1,0:T(8,128)S(1)}, u32[]{:S(2)}, u32[]{:S(2)}) collective-permute-start(f32[6,128]{1,0:T(8,128)S(1)} %get-tuple-element.35), channel_id=1, source_target_pairs={{0,1},{1,0},{2,3},{3,2},{4,5},{5,4},{6,7},{7,6},{8,9},{9,8},{10,11... | collective-permute-start | bytes 9224 | tf_op jit(solution)/shard_map/ppermute | solution.py:567
  83.3 0.6 copy-start.6
  83.9 0.6 copy-start.7

commit v4 on v3

--- a/solution.py
+++ b/solution.py
@@ -114,56 +114,56 @@
 
 def pair_sums(steps, units, base_of, finish, left_ref, right_ref, e0_ref, e1_ref, w0_ref, w1_ref):
     n = CELL_ATOMS
-
-    def powers(step, e_ref):
+    starts = [sum(len(others) for _, _, others in units[:k]) for k in range(len(units))]
+
+    def powers(k, step, e_ref):
         base = base_of(step)
-        at = 0
-        for _, center, others in units:
-            for offset, delta in others:
-                e_ref[at * n : (at + 1) * n] = jnp.dot(
-                    left_ref[base + offset],
-                    right_ref[base + center, 1 - delta],
-                    preferred_element_type=jnp.float32,
-                )
-                at += 1
-
-    def weights(e_ref, w_ref):
-        at = 0
-        for _, _, others in units:
-            for number in range(len(others)):
-                weight = jnp.exp2(e_ref[(at + number) * n : (at + number + 1) * n])
-                high = weight.astype(jnp.bfloat16)
-                low = (weight - high.astype(jnp.float32)).astype(jnp.bfloat16)
-                place = 2 * at + number
-                w_ref[place * n : (place + 1) * n] = high
-                place += len(others)
-                w_ref[place * n : (place + 1) * n] = low
-            at += len(others)
-
-    def sums(step, w_ref):
-        base = base_of(step)
-        at = 0
-        for tag, _, others in units:
-            rows = [right_ref[base + offset, delta + 1, 0:16] for offset, delta in others]
-            total = jnp.dot(
-                jnp.concatenate(rows + rows, axis=1),
-                w_ref[2 * at * n : 2 * (at + len(others)) * n],
+        _, center, others = units[k]
+        for number, (offset, delta) in enumerate(others):
+            at = starts[k] + number
+            e_ref[at * n : (at + 1) * n] = jnp.dot(
+                left_ref[base + offset],
+                right_ref[base + center, 1 - delta],
                 preferred_element_type=jnp.float32,
             )
-            finish(step, tag, total[:8] + total[8:])
-            at += len(others)
+
+    def weights(k, e_ref, w_ref):
+        count = len(units[k][2])
+        for number in range(count):
+            at = starts[k] + number
+            weight = jnp.exp2(e_ref[at * n : (at + 1) * n])
+            high = weight.astype(jnp.bfloat16)
+            low = (weight - high.astype(jnp.float32)).astype(jnp.bfloat16)
+            place = 2 * starts[k] + number
+            w_ref[place * n : (place + 1) * n] = high
+            place += count
+            w_ref[place * n : (place + 1) * n] = low
+
+    def sums(k, step, w_ref):
+        base = base_of(step)
+        tag, _, others = units[k]
+        rows = [right_ref[base + offset, delta + 1, 0:16] for offset, delta in others]
+        at = starts[k]
+        total = jnp.dot(
+            jnp.concatenate(rows + rows, axis=1),
+            w_ref[2 * at * n : 2 * (at + len(others)) * n],
+            preferred_element_type=jnp.float32,
+        )
+        finish(step, tag, total[:8] + total[8:])
 
     def clamp(step):
         return jnp.clip(step, 0, steps - 1)
 
     def pair(i, carry):
         step = 2 * i
-        sums(clamp(step - 2), w0_ref)
-        weights(e1_ref, w1_ref)
-        powers(clamp(step), e0_ref)
-        sums(clamp(step - 1), w1_ref)
-        weights(e0_ref, w0_ref)
-        powers(clamp(step + 1), e1_ref)
+        for first, e_new, e_old, w_new, w_old in (
+            (step, e0_ref, e1_ref, w1_ref, w0_ref),
+            (step + 1, e1_ref, e0_ref, w0_ref, w1_ref),
+        ):
+            for k in range(len(units)):
+                powers(k, clamp(first), e_new)
+                weights(k, e_old, w_new)
+                sums(k, clamp(first - 2), w_old)
         return carry
 
     lax.fori_loop(0, (steps + 3) // 2, pair, 0)
@@ -209,7 +209,7 @@
     return [(t, c, slice((t * 3 + c) * LANES, (t * 3 + c + 1) * LANES)) for t in range(tiles) for c in range(3)]
 
 
-def noise_kernel(drift_ref, mix_ref, aux_ref, noise_ref, first_ref, later_ref, rows_ref):
+def noise_kernel(drift_ref, mix_ref, aux_ref, noise_ref, first_ref, later0_ref, later_ref, rows_ref):
     beads = aux_ref.shape[0]
     size = AUX + 1
     tiles = aux_ref.shape[3] // LANES
@@ -245,7 +245,10 @@
             total = mixed(1, a, c, inner)
             for b in range(1, size):
                 total = total + drift[:, a * size + b : a * size + b + 1] * news[b]
-            later_ref[a, :, lanes] = total
+            if a == 0:
+                later0_ref[:, lanes] = total
+            else:
+                later_ref[a - 1, :, lanes] = total
 
 
 def twice(drift, a):
@@ -402,7 +405,7 @@
         pm = pm_ref[:, lanes]
         for a in range(1, size):
             rows_ref[c, t, pl.ds(a - 1, beads, stride=AUX), :] = drift[:, a * size : a * size + 1] * pm + (
-                again[a - 1] * pm1 + later_ref[a, :, lanes]
+                again[a - 1] * pm1 + later_ref[a - 1, :, lanes]
             )
 
     def copy(k, carry):
@@ -497,9 +500,9 @@
     )(by_coord(positions), by_coord(momenta), by_coord(forces))
     got = exchanged(send)
     rows = pltpu.VMEM((3, 2 * span, beads * AUX, LANES), jnp.float32)
-    first, later = call(
+    first, later0, later = call(
         noise_kernel,
-        [f32(beads, width), f32(size, beads, width)],
+        [f32(beads, width), f32(beads, width), f32(AUX, beads, width)],
         [VMEM_SPEC] * 4,
         scratch_shapes=[rows],
     )(drift, mix, jnp.transpose(aux_momenta, (0, 2, 1, 3)), jnp.transpose(noise, (0, 2, 3, 1, 4)))
@@ -529,7 +532,7 @@
 
     slots = 2 * beads * (span + 2)
     inside, outside = [], []
-    inside_runs, outside_runs = math.gcd(2 * beads, 4), math.gcd(2 * beads, 8)
+    inside_runs, outside_runs = math.gcd(2 * beads, 8), math.gcd(2 * beads, 8)
     for runs, units, near in ((inside_runs, inside, range(span)), (outside_runs, outside, (-1, span))):
         for run in range(runs):
             for u in range(span):
@@ -552,7 +555,7 @@
             pltpu.VMEM((2, span, beads * 8, LANES), jnp.float32),
         ]
         + pair_scratch(slots, outside),
-    )(own, part, up0, up1, dn0, dn1, qn, pn, pm, later[0], gather, basis, turn, drift)
+    )(own, part, up0, up1, dn0, dn1, qn, pn, pm, later0, gather, basis, turn, drift)
     got = exchanged(send)
     aux_out = call(
         functools.partial(rest_kernel, span=span),
@@ -560,13 +563,14 @@
         [VMEM_SPEC] * 4,
         scratch_shapes=[rows],
     )(pm, pm2, later, drift)
+    got, aux_out = lax.optimization_barrier((got, aux_out))
 
     head = got[: 3 * here]
     end = (2 * groups - 1) * here * columns
     tail = got[end - 3 * here : end]
     before = lax.ppermute(tail, "space", [(s, (s + 1) % spaces) for s in range(spaces)])
     after = lax.ppermute(head, "space", [(s, (s - 1) % spaces) for s in range(spaces)])
-    block = math.gcd(cells, 4)
+    block = math.gcd(cells, 8)
     around = [(u, u + 1, [(u, -1), (u + 1, 0), (u + 2, 1)]) for u in range(block)]
     new_q, new_p, new_f = call(
         functools.partial(bead_kernel, groups=groups, span=span, block=block, units=around),

time: 103 us -> 93.9 us (0.912)
  blocking collectives: 16.1 us -> 0 us
  waiting for transfers between devices: 5.16 us -> 15.5 us
  Pallas kernels: 58 us -> 52.5 us
  starting transfers between devices: 15.7 us -> 19.2 us
  local copies, waits for them, and re-layouts: 7 us -> 5.23 us
    all_to_all x1 -> x0, blocking collectives: 16.1 us -> none  [exchanged(): lax.all_to_all(block, 'bead', split_axis=0, concat_axis=0, tiled=True)]
    all_to_all x1 -> x2, waiting for transfers between devices: 5.14 us -> 14.7 us  [exchanged(): lax.all_to_all(block, 'bead', split_axis=0, concat_axis=0, tiled=True)]
    all_to_all x1 -> x2, starting transfers between devices: 8.34 us -> 11.9 us  [exchanged(): lax.all_to_all(block, 'bead', split_axis=0, concat_axis=0, tiled=True)]
    pallas_call x1, Pallas kernels: 14.6 us -> 12.4 us  [on_device(): call(functools.partial(inner_kernel, span=span, runs=inside_runs, units=i...]
    pallas_call x1, Pallas kernels: 18.1 us -> 16.2 us  [on_device(): call(functools.partial(bead_kernel, groups=groups, span=span, block=block...]
    squeeze x1 -> x0, local copies, waits for them, and re-layouts: 1.62 us -> none  [on_device(): later[0]]
    pallas_call x1, Pallas kernels: 12.6 us -> 11.4 us  [on_device(): call(functools.partial(outer_kernel, groups=groups, span=span, runs=outsi...]
  transfers between devices with their start and end apart: 7 -> 8, of which waited for: 1 -> 4; matrix products, arithmetic and copies ran while one was open for 4% -> 3% of each run, Pallas kernels for 22% -> 21%
where the time goes in v4:
time: 93.9 us; the launch traced here: 93.3 us
  Pallas kernels  52.5 us (56%)
  starting transfers between devices  19.2 us (20%)
  waiting for transfers between devices  15.5 us (17%)
  local copies, waits for them, and re-layouts  5.23 us (6%)
    pallas_call x1, Pallas kernels, on_device(): call(functools.partial(bead_kernel, groups=groups, span=span, block=block...  16.2 us
    all_to_all x2, waiting for transfers between devices, exchanged(): lax.all_to_all(block, 'bead', split_axis=0, concat_axis=0, tiled=True)  14.7 us
    pallas_call x1, Pallas kernels, on_device(): call(functools.partial(inner_kernel, span=span, runs=inside_runs, units=i...  12.4 us
    all_to_all x2, starting transfers between devices, exchanged(): lax.all_to_all(block, 'bead', split_axis=0, concat_axis=0, tiled=True)  11.9 us
    pallas_call x1, Pallas kernels, on_device(): call(functools.partial(outer_kernel, groups=groups, span=span, runs=outsi...  11.4 us
    ppermute x4, starting transfers between devices, shifted(): return lax.ppermute(block, ('bead', 'space'), route)  6.85 us
    pallas_call x1, Pallas kernels, on_device(): call(noise_kernel, [f32(beads, width), f32(beads, width), f32(AUX, beads,...  4.64 us
    pallas_call x1, Pallas kernels, on_device(): call(functools.partial(rest_kernel, span=span), f32(beads, 3, AUX, aux_mo...  2.98 us
  transfers between devices with their start and end apart: 8, of which 4 were waited for; matrix products, arithmetic and copies ran while one was open for 3% of the time, Pallas kernels for 21%

profile of v4, /device:TPU:0, one launch (start us, length us, event | category | flops | bytes accessed | tf_op | source)
XLA Modules:
  0.0 93.3 jit_solution(7036803245859786043)
XLA Ops:
  0.6 2.3 %shard_map.129 = f32[768,128]{1,0:T(8,128)} custom-call(f32[3,2,8192]{2,1,0:T(2,128)} %bitcast.26, f32[3,2,8192]{2,1,0:T(2,128)} %bitcast.27, f32[3,2,8192]{2,1,0:T(2,128)} %bitcast.28), custom_call_target="tpu_custom_call" | custom-call | tf_op jit(solution)/shard_map/pallas_call | solution.py:496
  2.9 8.3 %all-to-all-start = ((f32[16,48,128]{2,1,0:T(8,128)}), f32[16,48,128]{2,1,0:T(8,128)S(1)}, u32[]{:S(2)}, u32[]{:S(2)}) async-start(f32[16,48,128]{2,1,0:T(8,128)} %bitcast.22), calls=%async_computation | async-start | bytes 786432 | tf_op jit(solution)/shard_map/all_to_all | solution.py:494
  11.2 0.7 reshape.22
  12.0 0.7 copy.16.drift_ref
  12.7 0.7 reshape.23
  13.4 0.7 copy.17.mix_ref
  14.1 4.6 %shard_map.130 = (f32[32,1536]{1,0:T(8,128)}, f32[32,1536]{1,0:T(8,128)}, f32[4,32,1536]{2,1,0:T(8,128)}) custom-call(f32[32,25]{1,0:T(8,128)} %copy.16.drift_ref, f32[32,25]{1,0:T(8,128)} %copy.17.mix_ref, f32[32,3,4,512]{3,2,1,0:T(4,128)} %bitcast.23, f32[2,5,3,32,512]{4,3,2,1,0:T(8,128)} %bitcast.18), custom_call_target="tpu_custom_call" | custom-call | tf_op jit(solution)/shard_map/pallas_call | solution.py:503
  18.7 5.1 %all-to-all-done = f32[16,48,128]{2,1,0:T(8,128)S(1)} async-done(((f32[16,48,128]{2,1,0:T(8,128)}), f32[16,48,128]{2,1,0:T(8,128)S(1)}, u32[]{:S(2)}, u32[]{:S(2)}) %all-to-all-start) | async-done | bytes 393248 | tf_op jit(solution)/shard_map/all_to_all | solution.py:494
  23.9 0.8 copy-done.1
  24.6 2.7 %shard_map.131 = (f32[2,2,256,128]{3,2,1,0:T(8,128)}, f32[96,128]{1,0:T(8,128)}, f32[96,128]{1,0:T(8,128)}, f32[96,128]{1,0:T(8,128)}, f32[96,128]{1,0:T(8,128)}...) custom-call(s32[1]{0:T(128)} %bitcast.flag_ref, f32[768,128]{1,0:T(8,128)} %bitcast.21, ...), custom_call_target="tpu_custom_call" | custom-call | tf_op jit(solution)/shard_map/pallas_call | solution.py:512
  27.3 0.6 collective-permute-start
  27.9 1.7 %collective-permute-start.1 = (f32[96,128]{1,0:T(8,128)}, f32[96,128]{1,0:T(8,128)S(1)}, u32[]{:S(2)}, u32[]{:S(2)}) collective-permute-start(f32[96,128]{1,0:T(8,128)} %get-tuple-element.25), channel_id=1, source_target_pairs={{0,2},{1,3},{2,4},{3,5},{4,6},{5,7},{6,8},{7,9},{8,10},{9,11},{10,... | collective-permute-start | bytes 147464 | tf_op jit(solution)/shard_map/ppermute | solution.py:526
  29.6 3.9 %collective-permute-start.2 = (f32[96,128]{1,0:T(8,128)}, f32[96,128]{1,0:T(8,128)S(1)}, u32[]{:S(2)}, u32[]{:S(2)}) collective-permute-start(f32[96,128]{1,0:T(8,128)} %get-tuple-element.26), channel_id=1, source_target_pairs={{0,30},{1,31},{2,0},{3,1},{4,2},{5,3},{6,4},{7,5},{8,6},{9,7},{10,... | collective-permute-start | bytes 147464 | tf_op jit(solution)/shard_map/ppermute | solution.py:526
  33.5 0.6 collective-permute-start.3
  34.1 12.4 %shard_map.132.part_ref = f32[2,2,256,128]{3,2,1,0:T(8,128)} custom-call(f32[2,2,256,128]{3,2,1,0:T(8,128)} %get-tuple-element.23.own_ref), custom_call_target="tpu_custom_call" | custom-call | tf_op jit(solution)/shard_map/pallas_call | solution.py:543
  46.5 0.0 collective-permute-done.up0_ref
  46.6 0.0 collective-permute-done.2.dn0_ref
  46.6 0.6 copy-done.2
  47.2 0.0 copy-done.3
  47.2 0.0 copy-done.4
  47.2 0.0 copy-done.5
  47.2 11.4 %shard_map.133 = (f32[768,128]{1,0:T(8,128)}, f32[32,1536]{1,0:T(8,128)}) custom-call(f32[2,2,256,128]{3,2,1,0:T(8,128)} %get-tuple-element.23.own_ref, f32[2,2,256,128]{3,2,1,0:T(8,128)} %shard_map.132.part_ref, f32[96,128]{1,0:T(8,128)} %copy-done.2, f32[96,128]{1,0:T(8,128)} %copy-done.3, f32[96,128]{1,0:T(8,128)} %copy-done.4, f32[96,128]{1,0:T(8,128)} %copy-done.5, ...), custom_call_target="tpu_custom_call" | custom-call | tf_op jit(solution)/shard_map/pallas_call | solution.py:549
  58.6 3.6 %all-to-all-start.1 = ((f32[16,48,128]{2,1,0:T(8,128)}), f32[16,48,128]{2,1,0:T(8,128)S(1)}, u32[]{:S(2)}, u32[]{:S(2)}) async-start(f32[16,48,128]{2,1,0:T(8,128)} %bitcast.25), calls=%async_computation.1 | async-start | bytes 786432 | tf_op jit(solution)/shard_map/all_to_all | solution.py:494
  62.2 3.0 %shard_map.134 = f32[32,3,4,512]{3,2,1,0:T(4,128)} custom-call(f32[32,1536]{1,0:T(8,128)} %get-tuple-element.30.pm1_ref, f32[32,1536]{1,0:T(8,128)} %get-tuple-element.33.pm_ref, f32[4,32,1536]{2,1,0:T(8,128)} %get-tuple-element.34.later_ref, f32[32,25]{1,0:T(8,128)} %copy.16.drift_ref), custom_call_target="tpu_custom_call" | custom-call | tf_op jit(solution)/shard_map/pallas_call | solution.py:560
  65.1 9.5 %all-to-all-done.1 = f32[16,48,128]{2,1,0:T(8,128)S(1)} async-done(((f32[16,48,128]{2,1,0:T(8,128)}), f32[16,48,128]{2,1,0:T(8,128)S(1)}, u32[]{:S(2)}, u32[]{:S(2)}) %all-to-all-start.1) | async-done | bytes 393248 | tf_op jit(solution)/shard_map/all_to_all | solution.py:494
  74.7 0.0 collective-permute-start.5
  74.7 0.5 collective-permute-start.4
  75.2 0.7 collective-permute-done.5.after_ref
  75.9 0.2 collective-permute-done.4.before_ref
  76.0 0.4 copy-done.6
  76.4 0.6 copy-done.7
  77.0 16.2 %shard_map.135 = (f32[3,2,8192]{2,1,0:T(2,128)}, f32[3,2,8192]{2,1,0:T(2,128)}, f32[3,2,8192]{2,1,0:T(2,128)}) custom-call(f32[768,128]{1,0:T(8,128)} %bitcast.20, f32[6,128]{1,0:T(8,128)} %copy-done.7, f32[6,128]{1,0:T(8,128)} %copy-done.6), custom_call_target="tpu_custom_call" | custom-call | tf_op jit(solution)/shard_map/pallas_call | solution.py:575
  (12 shorter events, 0.0 us)
Async XLA Ops:
  2.9 21.0 %all-to-all-start = ((f32[16,48,128]{2,1,0:T(8,128)}), f32[16,48,128]{2,1,0:T(8,128)S(1)}, u32[]{:S(2)}, u32[]{:S(2)}) async-start(f32[16,48,128]{2,1,0:T(8,128)} %bitcast.22), calls=%async_computation | async-start | bytes 786432 | tf_op jit(solution)/shard_map/all_to_all | solution.py:494
  23.9 0.8 copy-start.1
  27.3 19.3 %collective-permute-start = (f32[96,128]{1,0:T(8,128)}, f32[96,128]{1,0:T(8,128)S(1)}, u32[]{:S(2)}, u32[]{:S(2)}) collective-permute-start(f32[96,128]{1,0:T(8,128)} %get-tuple-element.24), channel_id=1, source_target_pairs={{0,2},{1,3},{2,4},{3,5},{4,6},{5,7},{6,8},{7,9},{8,10},{9,11},{10,... | collective-permute-start | bytes 147464 | tf_op jit(solution)/shard_map/ppermute | solution.py:526
  27.9 18.7 %collective-permute-start.1 = (f32[96,128]{1,0:T(8,128)}, f32[96,128]{1,0:T(8,128)S(1)}, u32[]{:S(2)}, u32[]{:S(2)}) collective-permute-start(f32[96,128]{1,0:T(8,128)} %get-tuple-element.25), channel_id=1, source_target_pairs={{0,2},{1,3},{2,4},{3,5},{4,6},{5,7},{6,8},{7,9},{8,10},{9,11},{10,... | collective-permute-start | bytes 147464 | tf_op jit(solution)/shard_map/ppermute | solution.py:526
  29.6 16.9 %collective-permute-start.2 = (f32[96,128]{1,0:T(8,128)}, f32[96,128]{1,0:T(8,128)S(1)}, u32[]{:S(2)}, u32[]{:S(2)}) collective-permute-start(f32[96,128]{1,0:T(8,128)} %get-tuple-element.26), channel_id=1, source_target_pairs={{0,30},{1,31},{2,0},{3,1},{4,2},{5,3},{6,4},{7,5},{8,6},{9,7},{10,... | collective-permute-start | bytes 147464 | tf_op jit(solution)/shard_map/ppermute | solution.py:526
  33.5 13.1 %collective-permute-start.3 = (f32[96,128]{1,0:T(8,128)}, f32[96,128]{1,0:T(8,128)S(1)}, u32[]{:S(2)}, u32[]{:S(2)}) collective-permute-start(f32[96,128]{1,0:T(8,128)} %get-tuple-element.27), channel_id=1, source_target_pairs={{0,31},{1,30},{2,0},{3,1},{4,2},{5,3},{6,4},{7,5},{8,6},{9,7},{10,... | collective-permute-start | bytes 147464 | tf_op jit(solution)/shard_map/ppermute | solution.py:526
  46.6 0.6 copy-start.2
  46.6 0.6 copy-start.3
  46.6 0.6 copy-start.4
  46.6 0.6 copy-start.5
  58.6 16.1 %all-to-all-start.1 = ((f32[16,48,128]{2,1,0:T(8,128)}), f32[16,48,128]{2,1,0:T(8,128)S(1)}, u32[]{:S(2)}, u32[]{:S(2)}) async-start(f32[16,48,128]{2,1,0:T(8,128)} %bitcast.25), calls=%async_computation.1 | async-start | bytes 786432 | tf_op jit(solution)/shard_map/all_to_all | solution.py:494
  74.7 1.3 %copy-start = (f32[16,48,128]{2,1,0:T(8,128)}, f32[16,48,128]{2,1,0:T(8,128)S(1)}, u32[]{:S(2)}) copy-start(f32[16,48,128]{2,1,0:T(8,128)S(1)} %all-to-all-done.1) | copy-start | bytes 1179652
  74.7 1.2 %collective-permute-start.5 = (f32[6,128]{1,0:T(8,128)S(1)}, f32[6,128]{1,0:T(8,128)S(1)}, u32[]{:S(2)}, u32[]{:S(2)}) collective-permute-start(f32[6,128]{1,0:T(8,128)S(1)} %get-tuple-element.40), channel_id=1, source_target_pairs={{0,1},{1,0},{2,3},{3,2},{4,5},{5,4},{6,7},{7,6},{8,9},{9,8},{10,11... | collective-permute-start | bytes 9224 | tf_op jit(solution)/shard_map/ppermute | solution.py:572
  74.7 1.3 %collective-permute-start.4 = (f32[6,128]{1,0:T(8,128)S(1)}, f32[6,128]{1,0:T(8,128)S(1)}, u32[]{:S(2)}, u32[]{:S(2)}) collective-permute-start(f32[6,128]{1,0:T(8,128)S(1)} %get-tuple-element.41), channel_id=1, source_target_pairs={{0,1},{1,0},{2,3},{3,2},{4,5},{5,4},{6,7},{7,6},{8,9},{9,8},{10,11... | collective-permute-start | bytes 9224 | tf_op jit(solution)/shard_map/ppermute | solution.py:571
  75.8 0.6 copy-start.6
  76.4 0.6 copy-start.7
